TPU v7x, 128 devices: a whole 4x4x4 slice. The times are simulated.
128 devices in a mesh: section: 16 (over y_lo, z, core), dp: 8 (over x, y_hi).
Axes of the slice: x: 4, y: 4 (y_hi: 2, y_lo: 2; y = y_hi * 2 + y_lo), z: 4, core: 2. Of those that a mesh axis runs over, the one named last changes fastest.
Arguments:
- first_acts: bfloat16 [16, 1024, 8192], P('section', 'dp'), may hold values from -6 to 6
- first_grads: bfloat16 [16, 1024, 8192], P('section', 'dp'), may hold values from -6 to 6
- last_acts: bfloat16 [16, 1024, 8192], P('section', 'dp'), may hold values from -6 to 6
- last_grads: bfloat16 [16, 1024, 8192], P('section', 'dp'), may hold values from -6 to 6
- doc_lengths: int32 [8, 16], P('dp'), may hold values from 1 to 32, 128 in all within a row
- block_owner: int32 [16], replicated, may hold values from 0 to 7, as said below
Outputs:
- act_factor: float32 [16, 8, 4, 512, 512], P('section', 'dp')
- grad_factor: float32 [16, 8, 4, 512, 512], P('section', 'dp')
- act_cross: float32 [16, 8, 4, 512, 512], P('section', 'dp')
- grad_cross: float32 [16, 8, 4, 512, 512], P('section', 'dp')
Inputs may be any that keep to these rules, and one draw needn't show every extreme that they name: `doc_lengths`: documents fill their group's 128 rows exactly and the longest is exactly 32 rows. `block_owner`: one owner holds exactly 4 blocks, one holds none, every other holds exactly 2; which ones is drawn, except that the first and the last group always own blocks.
All inputs are finite; a program needn't handle non-finite values.
Results may differ from a plain program's by a relative error of at most 0.0037.
Values may be sent and summed in bfloat16 or wider, within the bound.
No kernel may reach another device: no remote copies, remote signals or barrier semaphores. Data moves between devices by JAX's collectives and lax.ppermute only.
A program may use at most 320 MiB of HBM per device.

v0:
```python
import functools

import jax
import jax.numpy as jnp
import numpy as np
from jax import lax
from jax.experimental import pallas as pl
from jax.experimental.pallas import tpu as pltpu
from jax.sharding import PartitionSpec as P

KEEP = 2
AXES = ("section", "dp")


def at(x, y):
    return (x % 4) * 2 + y


def patterns(route):
    if route == 0:
        return [{at(x, y): at(x + step, y) for x in range(4) for y in range(2)} for step in (1, -1)]
    xf, yf = (route - 1) // 2, (route - 1) % 2
    near = 1 - yf
    plus = {at(x, near): at(x + 1, near) for x in range(4)}
    plus[at(xf, near)] = at(xf, yf)
    minus = {at(x, near): at(x - 1, near) for x in range(4)}
    minus[at(xf + 1, near)] = at(xf + 1, yf)
    minus[at(xf + 1, yf)] = at(xf, yf)
    return [plus, minus]


def chains(spare, full):
    ways = []
    for step in patterns(0 if spare % 2 == full % 2 else 1 + full):
        between = [step[spare]]
        while between[-1] != full:
            between.append(step[between[-1]])
        ways.append(between[:-1])
    return ways


def plan_table(groups):
    table = np.zeros((groups * groups, 16), np.int32)
    for spare, full in [(s, f) for s in range(1, groups - 1) for f in range(groups) if f != s]:
        row = table[spare * groups + full]
        row[:groups] = np.arange(groups) * KEEP + 1
        for way, between in enumerate(chains(spare, full)):
            slot = spare * KEEP + way
            for g in between:
                row[g] = slot
                slot = g * KEEP + 1
                row[groups + 2 + way] |= 1 << g
            row[groups + way] = slot
        row[groups + 4] = 0 if spare % 2 == full % 2 else 1 + full
    return table.reshape(-1)


def prepare_kernel(groups, split, lengths, owner, table, one, two, *refs):
    outs, (meta, order, slots, counts) = refs[:-4], refs[-4:]
    blocks = owner.shape[0]
    step = pl.program_id(0)
    me = lax.axis_index("dp")

    @pl.when(step == 0)
    def _():
        for g in range(groups):
            counts[g] = 0
        for b in range(blocks):
            o = owner[b]
            slots[b] = counts[o]
            counts[o] = counts[o] + 1
        spare, full = jnp.int32(0), jnp.int32(0)
        for g in range(groups):
            spare = jnp.where(counts[g] == 0, g, spare)
            full = jnp.where(counts[g] > KEEP, g, full)
        row = (spare * groups + full) * 16
        for b in range(blocks):
            o, k = owner[b], slots[b]
            at = jnp.where(k <= 1, o, groups + jnp.minimum(k, 3) - 2)
            place = jnp.where(k == 0, o * KEEP, table[row + at])
            order[place] = b
        on_a = (table[row + groups + 2] >> me) & 1
        on_b = (table[row + groups + 3] >> me) & 1
        last = (me == full).astype(jnp.int32)
        meta[0] = (me == spare).astype(jnp.int32)
        meta[1] = on_a | on_b
        meta[2] = on_a + 2 * last
        meta[3] = on_b + 3 * last
        meta[4] = table[row + groups + 4]

    rows, width = one.shape
    feat = width // blocks
    row_at = lax.broadcasted_iota(jnp.int32, (rows, feat), 0) + step * rows
    length = jnp.ones((rows, feat), jnp.float32)
    start = jnp.int32(0)
    for d in range(lengths.shape[1]):
        size = lengths[0, d]
        inside = (row_at >= start) & (row_at < start + size)
        length = jnp.where(inside, size.astype(jnp.float32), length)
        start = start + size
    weight = jnp.sqrt((1.0 / length) / (lengths.shape[1] * groups))
    half = me % 2
    for x in range(groups // 2):
        for t in range(2):
            for k in range(KEEP):
                source = order[x * 4 + (half ^ t) * KEEP + k]
                columns = pl.ds(pl.multiple_of(source * feat, feat), feat)
                for a, ref in ((0, one), (1, two)):
                    value = (ref[:, columns].astype(jnp.float32) * weight).astype(jnp.bfloat16)
                    if split:
                        outs[t][x, a, k] = value
                    else:
                        outs[0][x, t, a, k] = value


def prepare(lengths, owner, table, one, two, groups, split):
    rows, width = one.shape
    feat = width // owner.shape[0]
    cut = rows // 4
    wide = groups // 2
    if split:
        shapes = [(wide, 2, KEEP, rows, feat)] * 2
    else:
        shapes = [(wide, 2, 2, KEEP, rows, feat)]
    smem = pl.BlockSpec(memory_space=pltpu.SMEM)
    take = pl.BlockSpec((cut, width), lambda i: (i, 0))

    def give(shape):
        lead = len(shape) - 2
        return pl.BlockSpec(shape[:lead] + (cut, feat), lambda i: (0,) * lead + (i, 0))

    return pl.pallas_call(
        functools.partial(prepare_kernel, groups, split),
        grid=(rows // cut,),
        in_specs=[smem, smem, smem, take, take],
        out_specs=[give(s) for s in shapes] + [smem],
        out_shape=[jax.ShapeDtypeStruct(s, jnp.bfloat16) for s in shapes]
        + [jax.ShapeDtypeStruct((8,), jnp.int32)],
        scratch_shapes=[
            pltpu.SMEM((owner.shape[0],), jnp.int32),
            pltpu.SMEM((owner.shape[0],), jnp.int32),
            pltpu.SMEM((groups,), jnp.int32),
        ],
        compiler_params=pltpu.CompilerParams(vmem_limit_bytes=60 << 20),
        name="prepare",
    )(lengths, owner, table, one, two)


def dot_rows(x, y):
    return lax.dot_general(x, y, (((0,), (0,)), ((), ())), preferred_element_type=jnp.float32)


def corners(matrix, symmetric):
    h = matrix.shape[0] // 2
    return [
        matrix[i * h : i * h + h, j * h : j * h + h].astype(jnp.bfloat16)
        for i in range(2)
        for j in range(2)
        if i <= j or not symmetric
    ]


def begin_kernel(own, last, *outs):
    k = pl.program_id(0)

    @pl.when(k < KEEP)
    def _():
        feat = own.shape[-1]
        for kind in range(2):
            f = own[:, 0, kind, 0].reshape(-1, feat)
            l = last[:, kind, 0].reshape(-1, feat)
            outs[2 * kind][0] = dot_rows(f, f)
            outs[2 * kind + 1][0] = dot_rows(l, f)

    @pl.when(k >= KEEP)
    def _():
        for out in outs:
            out[...] = jnp.zeros_like(out)


def begin(f_in, l_in):
    wide, _, _, _, rows, feat = f_in.shape
    at = lambda k: jnp.minimum(k, KEEP - 1)
    return pl.pallas_call(
        begin_kernel,
        grid=(2 * KEEP,),
        in_specs=[
            pl.BlockSpec((wide, 1, 2, 1, rows, feat), lambda k: (0, 0, 0, at(k), 0, 0)),
            pl.BlockSpec((wide, 2, 1, rows, feat), lambda k: (0, 0, at(k), 0, 0)),
        ],
        out_specs=[pl.BlockSpec((1, feat, feat), lambda k: (k, 0, 0))] * 4,
        out_shape=[jax.ShapeDtypeStruct((2 * KEEP, feat, feat), jnp.float32)] * 4,
        compiler_params=pltpu.CompilerParams(vmem_limit_bytes=60 << 20),
        name="begin",
    )(f_in, l_in)


def finish_kernel(symmetric, base, meta, *refs):
    ins, sums, ways = refs[: 1 if symmetric else 2], refs[-8:-6], refs[-4:-2]
    outs, (packed, sem) = refs[-6:-4], refs[-2:]
    k = pl.program_id(0)
    feat = ins[0].shape[-1]
    spare = meta[0] != 0
    foreign = spare | ((meta[1] != 0) & (k == 1))
    each = 3 if symmetric else 4
    for kind in range(2):
        f = ins[-1][:, kind, 0].reshape(-1, feat)
        l = ins[0][:, kind, 0].reshape(-1, feat)
        total = sums[kind][0] + dot_rows(l, f)
        outs[kind][0] = jnp.where(foreign, 0.0, total)

        @pl.when(foreign)
        def _():
            pieces = corners(total, symmetric)
            for way, chosen in ((0, spare == (k == 0)), (1, k == 1)):

                @pl.when(chosen)
                def _():
                    for n, piece in enumerate(pieces):
                        packed[way, each * kind + n] = piece

    @pl.when(foreign & (k == 1))
    def _():
        copies = [
            pltpu.make_async_copy(packed.at[way], ways[way].at[pl.ds(base, 2 * each)], sem.at[way])
            for way in range(2)
        ]
        for copy in copies:
            copy.start()
        for copy in copies:
            copy.wait()


def finish(meta, f_swap, l_in, sums, ways):
    symmetric = l_in is None
    ins = [f_swap] if symmetric else [l_in, f_swap]
    wide, _, _, rows, feat = f_swap.shape
    each, base = (3, 0) if symmetric else (4, 6)
    way = jax.ShapeDtypeStruct((14, feat // 2, feat // 2), jnp.bfloat16)
    out = jax.ShapeDtypeStruct((2 * KEEP, feat, feat), jnp.float32)
    block = pl.BlockSpec((1, feat, feat), lambda k, m: (k, 0, 0))
    anywhere = pl.BlockSpec(memory_space=pl.ANY)
    aliases = {1 + len(ins) + len(ways) + n: n for n in range(2)}
    aliases.update({1 + len(ins) + n: 2 + n for n in range(len(ways))})
    return pl.pallas_call(
        functools.partial(finish_kernel, symmetric, base),
        grid_spec=pltpu.PrefetchScalarGridSpec(
            num_scalar_prefetch=1,
            grid=(KEEP,),
            in_specs=[pl.BlockSpec((wide, 2, 1, rows, feat), lambda k, m: (0, 0, k, 0, 0))] * len(ins)
            + [anywhere] * len(ways)
            + [block] * 2,
            out_specs=[block] * 2 + [anywhere] * 2,
            scratch_shapes=[
                pltpu.VMEM((2, 2 * each, feat // 2, feat // 2), jnp.bfloat16),
                pltpu.SemaphoreType.DMA((2,)),
            ],
        ),
        out_shape=[out, out, way, way],
        input_output_aliases=aliases,
        compiler_params=pltpu.CompilerParams(vmem_limit_bytes=60 << 20),
        name="finish",
    )(meta, *ins, *ways, *sums)


def fill_kernel(meta, *refs):
    ways, outs, (half, wide, load_sem, store_sem) = refs[:2], refs[6:10], refs[10:]
    feat = wide.shape[-1]
    h = feat // 2
    slots = [meta[2], meta[3]]
    loads = [pltpu.make_async_copy(ways[w], half.at[w], load_sem.at[w]) for w in range(2)]

    def stores(w):
        return [
            pltpu.make_async_copy(wide.at[w, n], outs[n].at[slots[w]], store_sem.at[w, n]) for n in range(4)
        ]

    for w in range(2):

        @pl.when(slots[w] != 0)
        def _():
            loads[w].start()

    for w in range(2):

        @pl.when(slots[w] != 0)
        def _():
            loads[w].wait()
            started = stores(w)
            for kind in range(2):
                for n, (i, j) in enumerate([(0, 0), (0, 1), (1, 1)]):
                    piece = half[w, 3 * kind + n].astype(jnp.float32)
                    wide[w, 2 * kind, i * h : i * h + h, j * h : j * h + h] = piece
                    if i != j:
                        wide[w, 2 * kind, j * h : j * h + h, i * h : i * h + h] = piece.T
                started[2 * kind].start()
                for n in range(4):
                    i, j = n // 2, n % 2
                    piece = half[w, 6 + 4 * kind + n].astype(jnp.float32)
                    wide[w, 2 * kind + 1, i * h : i * h + h, j * h : j * h + h] = piece
                started[2 * kind + 1].start()

    for w in range(2):

        @pl.when(slots[w] != 0)
        def _():
            for store in stores(w):
                store.wait()


def fill(meta, way_a, way_b, outs):
    feat = outs[0].shape[-1]
    anywhere = pl.BlockSpec(memory_space=pl.ANY)
    return pl.pallas_call(
        fill_kernel,
        in_specs=[pl.BlockSpec(memory_space=pltpu.SMEM)] + [anywhere] * 6,
        out_specs=[anywhere] * 4,
        out_shape=[jax.ShapeDtypeStruct(o.shape, o.dtype) for o in outs],
        scratch_shapes=[
            pltpu.VMEM((2,) + way_a.shape, jnp.bfloat16),
            pltpu.VMEM((2, 4, feat, feat), jnp.float32),
            pltpu.SemaphoreType.DMA((2,)),
            pltpu.SemaphoreType.DMA((2, 4)),
        ],
        input_output_aliases={3 + n: n for n in range(4)},
        compiler_params=pltpu.CompilerParams(vmem_limit_bytes=60 << 20),
        name="fill_slots",
    )(meta, way_a, way_b, *outs)


def hand_over(route, groups, way_a, way_b):
    sections = lax.axis_size("section")

    def along(number, *values):
        sent = []
        for value, step in zip(values, patterns(number)):
            pairs = [(s * groups + i, s * groups + j) for s in range(sections) for i, j in step.items()]
            sent.append(lax.ppermute(value, AXES, pairs))
        return tuple(sent)

    return lax.switch(route, [functools.partial(along, n) for n in range(groups + 1)], way_a, way_b)


def on_device(first_acts, first_grads, last_acts, last_grads, doc_lengths, block_owner):
    groups = lax.axis_size("dp")
    sections = lax.axis_size("section")
    table = jnp.asarray(plan_table(groups))
    f, meta = prepare(doc_lengths, block_owner, table, first_acts[0], first_grads[0], groups, False)
    meta, last_acts, last_grads = lax.optimization_barrier((meta, last_acts, last_grads))
    l_own, l_other, _ = prepare(doc_lengths, block_owner, table, last_acts[0], last_grads[0], groups, True)

    straight = [(s * groups + d, (s + 1) * groups + d) for s in range(sections - 1) for d in range(groups)]
    across = [(i, j ^ 1) for i, j in straight]
    swap = [(i, i ^ 1) for i in range(sections * groups)]
    rows_of = [[d for d in range(groups) if d % 2 == y] for y in range(2)]

    def exchange(x):
        return lax.all_to_all(x, "dp", split_axis=0, concat_axis=0, tiled=True, axis_index_groups=rows_of)

    l_own = lax.ppermute(l_own, AXES, straight)
    l_other = lax.ppermute(l_other, AXES, across)
    f_in = exchange(f)
    f_in, l_own = lax.optimization_barrier((f_in, l_own))
    f_swap = lax.ppermute(f_in[:, 1], AXES, swap)
    l_own = exchange(l_own)
    l_own, l_other = lax.optimization_barrier((l_own, l_other))
    l_other = exchange(l_other)
    af, ac, gf, gc = begin(f_in, l_own)
    af, gf, *ways = finish(meta, f_swap, None, (af, gf), ())
    ac, gc, *ways = finish(meta, f_swap, l_other, (ac, gc), ways)
    got = hand_over(meta[4], groups, *ways)
    af, ac, gf, gc = fill(meta, *got, (af, ac, gf, gc))
    return af[None, None], gf[None, None], ac[None, None], gc[None, None]


def solution(mesh):
    placed = (
        P("section", "dp", None),
        P("section", "dp", None),
        P("section", "dp", None),
        P("section", "dp", None),
        P("dp", None),
        P(),
    )
    return jax.shard_map(
        on_device,
        mesh=mesh,
        in_specs=placed,
        out_specs=(P("section", "dp", None, None, None),) * 4,
        check_vma=False,
    )
```

profile of v0, /device:TPU:30, one launch (start us, length us, event | category | flops | bytes accessed | tf_op | source)
XLA Modules:
  0.0 200.4 jit_solution(1180682512493379254)
XLA Ops:
  0.6 5.2 %prepare.2 = (bf16[4,2,2,2,128,512]{5,4,3,2,1,0:T(8,128)(2,1)}, s32[8]{0:T(128)}) custom-call(s32[1,16]{1,0:T(1,128)} %lengths.3, s32[16]{0:T(128)} %owner.3, s32[1024]{0:T(1024)} %constant.8.clone.table, bf16[128,8192]{1,0:T(8,128)(2,1)} %bitcast.15, bf16[128,8192]{1,0:T(8,128)(2,1)} %bitcast.16), custom_call_target="tpu_custom_call" | custom-call | tf_op jit(solution)/shard_map/prepare/pallas_call | solution.py:132
  5.8 5.3 %all-to-all-start = ((bf16[4,2,2,2,128,512]{5,4,3,2,1,0:T(8,128)(2,1)}), bf16[4,2,2,2,128,512]{5,4,3,2,1,0:T(8,128)(2,1)}, u32[]{:S(2)}, u32[]{:S(2)}) async-start(bf16[4,2,2,2,128,512]{5,4,3,2,1,0:T(8,128)(2,1)} %get-tuple-element.89), calls=%async_computation | async-start | bytes 8388608 | tf_op jit(solution)/shard_map/all_to_all | solution.py:358
  11.1 5.1 %prepare.3 = (bf16[4,2,2,128,512]{4,3,2,1,0:T(8,128)(2,1)}, bf16[4,2,2,128,512]{4,3,2,1,0:T(8,128)(2,1)}, s32[8]{0:T(128)}) custom-call(s32[1,16]{1,0:T(1,128)} %lengths.3, s32[16]{0:T(128)} %owner.3, s32[1024]{0:T(1024)} %constant.8.clone.table, bf16[128,8192]{1,0:T(8,128)(2,1)} %bitcast.17, bf16[128,8192]{1,0:T(8,128)(2,1)} %bitcast.18), custom_call_target="tpu_custom_call" | custom-call | tf_op jit(solution)/shard_map/prepare/pallas_call | solution.py:132
  16.2 1.9 collective-permute-start.18
  18.1 4.8 %collective-permute-start.19 = (bf16[4,2,2,128,512]{4,3,2,1,0:T(8,128)(2,1)}, bf16[4,2,2,128,512]{4,3,2,1,0:T(8,128)(2,1)}, u32[]{:S(2)}, u32[]{:S(2)}) collective-permute-start(bf16[4,2,2,128,512]{4,3,2,1,0:T(8,128)(2,1)} %get-tuple-element.94), channel_id=1, source_target_pairs={{0,9},{1,8},{2,11},{3,10},{4,13},{5,12},{6,15},{7,14},{8,17},{9,16... | collective-permute-start | bytes 6291464 | tf_op jit(solution)/shard_map/ppermute | solution.py:361
  22.9 47.0 %collective-permute-done.18 = bf16[4,2,2,128,512]{4,3,2,1,0:T(8,128)(2,1)S(1)} collective-permute-done((bf16[4,2,2,128,512]{4,3,2,1,0:T(8,128)(2,1)}, bf16[4,2,2,128,512]{4,3,2,1,0:T(8,128)(2,1)S(1)}, u32[]{:S(2)}, u32[]{:S(2)}) %collective-permute-start.18) | collective-permute-done | bytes 2097184 | tf_op jit(solution)/shard_map/ppermute | solution.py:360
  69.8 1.3 copy-done.2
  71.2 4.8 %all-to-all-start.1 = ((bf16[4,2,2,128,512]{4,3,2,1,0:T(8,128)(2,1)}), bf16[4,2,2,128,512]{4,3,2,1,0:T(8,128)(2,1)S(1)}, u32[]{:S(2)}, u32[]{:S(2)}) async-start(bf16[4,2,2,128,512]{4,3,2,1,0:T(8,128)(2,1)} %copy-done.2), calls=%async_computation.1 | async-start | bytes 4194304 | tf_op jit(solution)/shard_map/all_to_all | solution.py:358
  76.0 3.2 %slice_bitcast_fusion = bf16[4,2,2,128,512]{4,3,2,1,0:T(8,128)(2,1)} fusion(bf16[4,2,2,2,128,512]{5,4,3,2,1,0:T(8,128)(2,1)} %all-to-all-done.own), kind=kLoop, calls=%fused_computation | loop fusion | bytes 4194304 | tf_op jit(solution)/shard_map/squeeze | solution.py:364
  79.1 45.1 %collective-permute-done.19 = bf16[4,2,2,128,512]{4,3,2,1,0:T(8,128)(2,1)} collective-permute-done((bf16[4,2,2,128,512]{4,3,2,1,0:T(8,128)(2,1)}, bf16[4,2,2,128,512]{4,3,2,1,0:T(8,128)(2,1)}, u32[]{:S(2)}, u32[]{:S(2)}) %collective-permute-start.19) | collective-permute-done | bytes 2097184 | tf_op jit(solution)/shard_map/ppermute | solution.py:361
  124.2 1.4 copy-done.1
  125.6 4.8 %all-to-all-start.2 = ((bf16[4,2,2,128,512]{4,3,2,1,0:T(8,128)(2,1)}), bf16[4,2,2,128,512]{4,3,2,1,0:T(8,128)(2,1)S(1)}, u32[]{:S(2)}, u32[]{:S(2)}) async-start(bf16[4,2,2,128,512]{4,3,2,1,0:T(8,128)(2,1)} %collective-permute-done.19), calls=%async_computation.2 | async-start | bytes 4194304 | tf_op jit(solution)/shard_map/all_to_all | solution.py:358
  130.4 0.6 slice.6
  131.6 8.7 %begin.1 = (f32[4,512,512]{2,1,0:T(8,128)}, f32[4,512,512]{2,1,0:T(8,128)}, f32[4,512,512]{2,1,0:T(8,128)}, f32[4,512,512]{2,1,0:T(8,128)}) custom-call(bf16[4,2,2,2,128,512]{5,4,3,2,1,0:T(8,128)(2,1)} %all-to-all-done.own, bf16[4,2,2,128,512]{4,3,2,1,0:T(8,128)(2,1)} %copy-done.1), custom_call_target="tpu_custom_call" | custom-call | tf_op jit(solution)/shard_map/begin/pallas_call | solution.py:184
  140.3 7.1 %finish.2 = (f32[4,512,512]{2,1,0:T(8,128)}, f32[4,512,512]{2,1,0:T(8,128)}, bf16[14,256,256]{2,1,0:T(8,128)(2,1)}, bf16[14,256,256]{2,1,0:T(8,128)(2,1)}) custom-call(s32[8]{0:T(128)} %get-tuple-element.88.meta, bf16[4,2,2,128,512]{4,3,2,1,0:T(8,128)(2,1)} %collective-permute-done.20.refs_0_.refs_1_, ...), custom_call_target="tpu_custom_call", output_to_operand_aliasing={{0}: (2, {}), {1}: (3, {})} | custom-call | tf_op jit(solution)/shard_map/finish/pallas_call | solution.py:245
  147.4 6.9 %all-to-all-done.2.refs_0_ = bf16[4,2,2,128,512]{4,3,2,1,0:T(8,128)(2,1)S(1)} async-done(((bf16[4,2,2,128,512]{4,3,2,1,0:T(8,128)(2,1)}), bf16[4,2,2,128,512]{4,3,2,1,0:T(8,128)(2,1)S(1)}, u32[]{:S(2)}, u32[]{:S(2)}) %all-to-all-start.2) | async-done | bytes 2097184 | tf_op jit(solution)/shard_map/all_to_all | solution.py:358
  154.3 1.4 copy-done
  155.6 7.9 %finish.3 = (f32[4,512,512]{2,1,0:T(8,128)}, f32[4,512,512]{2,1,0:T(8,128)}, bf16[14,256,256]{2,1,0:T(8,128)(2,1)}, bf16[14,256,256]{2,1,0:T(8,128)(2,1)}) custom-call(s32[8]{0:T(128)} %get-tuple-element.88.meta, bf16[4,2,2,128,512]{4,3,2,1,0:T(8,128)(2,1)} %copy-done, ...), custom_call_target="tpu_custom_call", output_to_operand_aliasing={{0}: (5, {}), {1}: (6, {}), {2}: (3, {}), {3}: (4, {})} | custom-call | tf_op jit(solution)/shard_map/finish/pallas_call | solution.py:245
  163.6 32.4 %conditional.1 = (bf16[14,256,256]{2,1,0:T(8,128)(2,1)}, bf16[14,256,256]{2,1,0:T(8,128)(2,1)}) conditional(s32[]{:T(128)} %bitcast.2, (bf16[14,256,256]{2,1,0:T(8,128)(2,1)}, bf16[14,256,256]{2,1,0:T(8,128)(2,1)}) %tuple.50, (bf16[14,256,256]{2,1,0:T(8,128)(2,1)}, bf16[14,256,256]{2,1,0:T(8,128)(2,1)}) %tuple.50, ...), branch_computations={%region_0.0_spmd, %region_1.0_spmd, %region_2.0_spmd, %region_3.0_... | conditional | bytes 14680160 | solution.py:341
  163.6 5.7 %collective-permute-start.6 = (bf16[14,256,256]{2,1,0:T(8,128)(2,1)}, bf16[14,256,256]{2,1,0:T(8,128)(2,1)}, u32[]{:S(2)}, u32[]{:S(2)}) collective-permute-start(bf16[14,256,256]{2,1,0:T(8,128)(2,1)} %get-tuple-element.42), channel_id=1, source_target_pairs={{1,3},{3,2},{5,7},{7,1},{9,11},{11,10},{13,15},{15,9},{17,19},{19,... | collective-permute-start | bytes 5505032 | tf_op jit(solution)/shard_map/cond/branch_3_fun/ppermute | solution.py:338
  169.3 1.9 collective-permute-start.7
  171.2 19.1 %collective-permute-done.6 = bf16[14,256,256]{2,1,0:T(8,128)(2,1)} collective-permute-done((bf16[14,256,256]{2,1,0:T(8,128)(2,1)}, bf16[14,256,256]{2,1,0:T(8,128)(2,1)}, u32[]{:S(2)}, u32[]{:S(2)}) %collective-permute-start.6) | collective-permute-done | bytes 1835040 | tf_op jit(solution)/shard_map/cond/branch_3_fun/ppermute | solution.py:338
  190.3 5.6 %collective-permute-done.7 = bf16[14,256,256]{2,1,0:T(8,128)(2,1)} collective-permute-done((bf16[14,256,256]{2,1,0:T(8,128)(2,1)}, bf16[14,256,256]{2,1,0:T(8,128)(2,1)}, u32[]{:S(2)}, u32[]{:S(2)}) %collective-permute-start.7) | collective-permute-done | bytes 1835040 | tf_op jit(solution)/shard_map/cond/branch_3_fun/ppermute | solution.py:338
  195.9 4.4 %fill_slots.1 = (f32[4,512,512]{2,1,0:T(8,128)}, f32[4,512,512]{2,1,0:T(8,128)}, f32[4,512,512]{2,1,0:T(8,128)}, f32[4,512,512]{2,1,0:T(8,128)}) custom-call(s32[8]{0:T(128)} %get-tuple-element.88.meta, bf16[14,256,256]{2,1,0:T(8,128)(2,1)} %get-tuple-element.106.refs_0_, ...), custom_call_target="tpu_custom_call", output_to_operand_aliasing={{0}: (3, {}), {1}: (4, {}), {2}: (5, {}), {3}: (6, {})} | custom-call | tf_op jit(solution)/shard_map/fill_slots/pallas_call | solution.py:314
  (9 shorter events, 0.0 us)
Async XLA Ops:
  5.8 65.4 %all-to-all-start = ((bf16[4,2,2,2,128,512]{5,4,3,2,1,0:T(8,128)(2,1)}), bf16[4,2,2,2,128,512]{5,4,3,2,1,0:T(8,128)(2,1)}, u32[]{:S(2)}, u32[]{:S(2)}) async-start(bf16[4,2,2,2,128,512]{5,4,3,2,1,0:T(8,128)(2,1)} %get-tuple-element.89), calls=%async_computation | async-start | bytes 8388608 | tf_op jit(solution)/shard_map/all_to_all | solution.py:358
  16.2 53.7 %collective-permute-start.18 = (bf16[4,2,2,128,512]{4,3,2,1,0:T(8,128)(2,1)}, bf16[4,2,2,128,512]{4,3,2,1,0:T(8,128)(2,1)S(1)}, u32[]{:S(2)}, u32[]{:S(2)}) collective-permute-start(bf16[4,2,2,128,512]{4,3,2,1,0:T(8,128)(2,1)} %get-tuple-element.92), channel_id=1, source_target_pairs={{0,8},{1,9},{2,10},{3,11},{4,12},{5,13},{6,14},{7,15},{8,16},{9,17... | collective-permute-start | bytes 6291464 | tf_op jit(solution)/shard_map/ppermute | solution.py:360
  18.1 106.1 %collective-permute-start.19 = (bf16[4,2,2,128,512]{4,3,2,1,0:T(8,128)(2,1)}, bf16[4,2,2,128,512]{4,3,2,1,0:T(8,128)(2,1)}, u32[]{:S(2)}, u32[]{:S(2)}) collective-permute-start(bf16[4,2,2,128,512]{4,3,2,1,0:T(8,128)(2,1)} %get-tuple-element.94), channel_id=1, source_target_pairs={{0,9},{1,8},{2,11},{3,10},{4,13},{5,12},{6,15},{7,14},{8,17},{9,16... | collective-permute-start | bytes 6291464 | tf_op jit(solution)/shard_map/ppermute | solution.py:361
  69.8 1.3 copy-start.2
  71.2 53.1 %all-to-all-start.1 = ((bf16[4,2,2,128,512]{4,3,2,1,0:T(8,128)(2,1)}), bf16[4,2,2,128,512]{4,3,2,1,0:T(8,128)(2,1)S(1)}, u32[]{:S(2)}, u32[]{:S(2)}) async-start(bf16[4,2,2,128,512]{4,3,2,1,0:T(8,128)(2,1)} %copy-done.2), calls=%async_computation.1 | async-start | bytes 4194304 | tf_op jit(solution)/shard_map/all_to_all | solution.py:358
  79.1 51.3 %copy-start.3 = (s32[8]{0:T(128)S(1)}, s32[8]{0:T(128)}, u32[]{:S(2)}) copy-start(s32[8]{0:T(128)} %get-tuple-element.88.meta) | copy-start | bytes 100
  79.1 61.2 %collective-permute-start.20 = (bf16[4,2,2,128,512]{4,3,2,1,0:T(8,128)(2,1)}, bf16[4,2,2,128,512]{4,3,2,1,0:T(8,128)(2,1)}, u32[]{:S(2)}, u32[]{:S(2)}) collective-permute-start(bf16[4,2,2,128,512]{4,3,2,1,0:T(8,128)(2,1)} %slice_bitcast_fusion), channel_id=1, source_target_pairs={{0,1},{1,0},{2,3},{3,2},{4,5},{5,4},{6,7},{7,6},{8,9},{9,8},{10,11... | collective-permute-start | bytes 6291464 | tf_op jit(solution)/shard_map/ppermute | solution.py:364
  124.2 1.4 copy-start.1
  125.6 28.7 %all-to-all-start.2 = ((bf16[4,2,2,128,512]{4,3,2,1,0:T(8,128)(2,1)}), bf16[4,2,2,128,512]{4,3,2,1,0:T(8,128)(2,1)S(1)}, u32[]{:S(2)}, u32[]{:S(2)}) async-start(bf16[4,2,2,128,512]{4,3,2,1,0:T(8,128)(2,1)} %collective-permute-done.19), calls=%async_computation.2 | async-start | bytes 4194304 | tf_op jit(solution)/shard_map/all_to_all | solution.py:358
  154.3 1.4 copy-start
  163.6 26.8 %collective-permute-start.6 = (bf16[14,256,256]{2,1,0:T(8,128)(2,1)}, bf16[14,256,256]{2,1,0:T(8,128)(2,1)}, u32[]{:S(2)}, u32[]{:S(2)}) collective-permute-start(bf16[14,256,256]{2,1,0:T(8,128)(2,1)} %get-tuple-element.42), channel_id=1, source_target_pairs={{1,3},{3,2},{5,7},{7,1},{9,11},{11,10},{13,15},{15,9},{17,19},{19,... | collective-permute-start | bytes 5505032 | tf_op jit(solution)/shard_map/cond/branch_3_fun/ppermute | solution.py:338
  169.3 26.6 %collective-permute-start.7 = (bf16[14,256,256]{2,1,0:T(8,128)(2,1)}, bf16[14,256,256]{2,1,0:T(8,128)(2,1)}, u32[]{:S(2)}, u32[]{:S(2)}) collective-permute-start(bf16[14,256,256]{2,1,0:T(8,128)(2,1)} %get-tuple-element.43), channel_id=1, source_target_pairs={{1,7},{3,1},{5,4},{7,5},{4,2},{9,15},{11,9},{13,12},{15,13},{12,10... | collective-permute-start | bytes 5505032 | tf_op jit(solution)/shard_map/cond/branch_3_fun/ppermute | solution.py:338
where the time goes:
time: 200 us
  waiting for transfers between devices  124 us (62%)
  Pallas kernels  38.4 us (19%)
  starting transfers between devices  29.2 us (15%)
  local copies, waits for them, and re-layouts  7.79 us (4%)
    ppermute x1, waiting for transfers between devices, on_device(): l_own = lax.ppermute(l_own, AXES, straight)  47 us
    ppermute x1, waiting for transfers between devices, on_device(): l_other = lax.ppermute(l_other, AXES, across)  45.1 us
    ppermute x2, waiting for transfers between devices, along(): sent.append(lax.ppermute(value, AXES, pairs))  24.7 us
    pallas_call x2, Pallas kernels, finish(): pl.pallas_call(functools.partial(finish_kernel, symmetric, base), grid_sp...  15 us
    all_to_all x3, starting transfers between devices, exchange(): lax.all_to_all(x, 'dp', split_axis=0, concat_axis=0, tiled=True, axis_ind...  14.9 us
    pallas_call x2, Pallas kernels, prepare(): pl.pallas_call(functools.partial(prepare_kernel, groups, split), grid=(ro...  10.3 us
    pallas_call x1, Pallas kernels, begin(): pl.pallas_call(begin_kernel, grid=(2 * KEEP,), in_specs=[pl.BlockSpec((wi...  8.68 us
    ppermute x2, starting transfers between devices, along(): sent.append(lax.ppermute(value, AXES, pairs))  7.63 us
  transfers between devices with their start and end apart: 8, of which 5 were waited for; matrix products, arithmetic and copies ran while one was open for 2% of the time, Pallas kernels for 10%

commit v1 on v0

--- a/solution.py
+++ b/solution.py
@@ -55,7 +55,7 @@
     return table.reshape(-1)
 
 
-def prepare_kernel(groups, split, lengths, owner, table, one, two, *refs):
+def prepare_kernel(groups, relative, lengths, owner, table, one, two, *refs):
     outs, (meta, order, slots, counts) = refs[:-4], refs[-4:]
     blocks = owner.shape[0]
     step = pl.program_id(0)
@@ -90,8 +90,9 @@
 
     rows, width = one.shape
     feat = width // blocks
-    row_at = lax.broadcasted_iota(jnp.int32, (rows, feat), 0) + step * rows
-    length = jnp.ones((rows, feat), jnp.float32)
+    lanes = 128
+    row_at = lax.broadcasted_iota(jnp.int32, (rows, lanes), 0) + step * rows
+    length = jnp.ones((rows, lanes), jnp.float32)
     start = jnp.int32(0)
     for d in range(lengths.shape[1]):
         size = lengths[0, d]
@@ -99,29 +100,25 @@
         length = jnp.where(inside, size.astype(jnp.float32), length)
         start = start + size
     weight = jnp.sqrt((1.0 / length) / (lengths.shape[1] * groups))
+    weight = jnp.concatenate([weight] * (feat // lanes), axis=1)
     half = me % 2
     for x in range(groups // 2):
         for t in range(2):
             for k in range(KEEP):
-                source = order[x * 4 + (half ^ t) * KEEP + k]
+                column = (me // 2 + x) % 4 if relative else x
+                source = order[column * 4 + (half ^ t) * KEEP + k]
                 columns = pl.ds(pl.multiple_of(source * feat, feat), feat)
                 for a, ref in ((0, one), (1, two)):
                     value = (ref[:, columns].astype(jnp.float32) * weight).astype(jnp.bfloat16)
-                    if split:
-                        outs[t][x, a, k] = value
-                    else:
-                        outs[0][x, t, a, k] = value
-
-
-def prepare(lengths, owner, table, one, two, groups, split):
+                    outs[t][x, a, k] = value
+
+
+def prepare(lengths, owner, table, one, two, groups, relative):
     rows, width = one.shape
     feat = width // owner.shape[0]
     cut = rows // 4
     wide = groups // 2
-    if split:
-        shapes = [(wide, 2, KEEP, rows, feat)] * 2
-    else:
-        shapes = [(wide, 2, 2, KEEP, rows, feat)]
+    shapes = [(wide, 2, KEEP, rows, feat)] * 2
     smem = pl.BlockSpec(memory_space=pltpu.SMEM)
     take = pl.BlockSpec((cut, width), lambda i: (i, 0))
 
@@ -130,7 +127,7 @@
         return pl.BlockSpec(shape[:lead] + (cut, feat), lambda i: (0,) * lead + (i, 0))
 
     return pl.pallas_call(
-        functools.partial(prepare_kernel, groups, split),
+        functools.partial(prepare_kernel, groups, relative),
         grid=(rows // cut,),
         in_specs=[smem, smem, smem, take, take],
         out_specs=[give(s) for s in shapes] + [smem],
@@ -150,25 +147,33 @@
     return lax.dot_general(x, y, (((0,), (0,)), ((), ())), preferred_element_type=jnp.float32)
 
 
-def corners(matrix, symmetric):
-    h = matrix.shape[0] // 2
-    return [
-        matrix[i * h : i * h + h, j * h : j * h + h].astype(jnp.bfloat16)
-        for i in range(2)
-        for j in range(2)
-        if i <= j or not symmetric
-    ]
-
-
-def begin_kernel(own, last, *outs):
+def symmetric_tiles(feat):
+    return [((0, 0), (0, 1)), ((0, 2), (0, 3)), ((1, 2), (1, 3)), ((1, 1), (3, 3)), ((2, 2), (2, 3))]
+
+
+def pack_symmetric(matrix):
+    h = matrix.shape[0] // 4
+    piece = lambda i, j: matrix[i * h : i * h + h, j * h : j * h + h]
+    return [jnp.concatenate([piece(*p), piece(*q)], axis=1) for p, q in symmetric_tiles(4 * h)]
+
+
+def pack_whole(matrix):
+    h, half = matrix.shape[0] // 4, matrix.shape[1] // 2
+    return [matrix[i * h : i * h + h, j * half : j * half + half] for i in range(4) for j in range(2)]
+
+
+def stack_rows(refs, kind):
+    return jnp.concatenate([ref[0, kind, 0] for ref in refs], axis=0)
+
+
+def begin_kernel(column, meta, *refs):
+    own, last, outs = refs[:4], refs[4:8], refs[8:]
     k = pl.program_id(0)
 
     @pl.when(k < KEEP)
     def _():
-        feat = own.shape[-1]
         for kind in range(2):
-            f = own[:, 0, kind, 0].reshape(-1, feat)
-            l = last[:, kind, 0].reshape(-1, feat)
+            f, l = stack_rows(own, kind), stack_rows(last, kind)
             outs[2 * kind][0] = dot_rows(f, f)
             outs[2 * kind + 1][0] = dot_rows(l, f)
 
@@ -178,95 +183,122 @@
             out[...] = jnp.zeros_like(out)
 
 
-def begin(f_in, l_in):
-    wide, _, _, _, rows, feat = f_in.shape
-    at = lambda k: jnp.minimum(k, KEEP - 1)
+def by_sender(shape, index_of):
+    wide, _, _, rows, feat = shape
+
+    def spec(back):
+        def index(*args):
+            kind, k = index_of(*args)
+            return ((args[-2][0] + wide - back) % wide, kind, k, 0, 0)
+
+        return index
+
+    return [spec(back) for back in range(wide)]
+
+
+def begin(column, meta, f_in, l_in):
+    wide, kinds, _, rows, feat = f_in.shape
+    low = lambda k, c, m: (0, jnp.minimum(k, KEEP - 1))
+    both = (1, kinds, 1, rows, feat)
+    received = lambda k, c, m: (0, 0, jnp.minimum(k, KEEP - 1), 0, 0)
     return pl.pallas_call(
         begin_kernel,
-        grid=(2 * KEEP,),
-        in_specs=[
-            pl.BlockSpec((wide, 1, 2, 1, rows, feat), lambda k: (0, 0, 0, at(k), 0, 0)),
-            pl.BlockSpec((wide, 2, 1, rows, feat), lambda k: (0, 0, at(k), 0, 0)),
-        ],
-        out_specs=[pl.BlockSpec((1, feat, feat), lambda k: (k, 0, 0))] * 4,
+        grid_spec=pltpu.PrefetchScalarGridSpec(
+            num_scalar_prefetch=2,
+            grid=(2 * KEEP,),
+            in_specs=[pl.BlockSpec(both, index) for index in by_sender(f_in.shape, low)]
+            + [pl.BlockSpec(both, received)] * wide,
+            out_specs=[pl.BlockSpec((1, feat, feat), lambda k, c, m: (k, 0, 0))] * 4,
+        ),
         out_shape=[jax.ShapeDtypeStruct((2 * KEEP, feat, feat), jnp.float32)] * 4,
-        compiler_params=pltpu.CompilerParams(vmem_limit_bytes=60 << 20),
+        compiler_params=pltpu.CompilerParams(vmem_limit_bytes=32 << 20),
         name="begin",
-    )(f_in, l_in)
-
-
-def finish_kernel(symmetric, base, meta, *refs):
-    ins, sums, ways = refs[: 1 if symmetric else 2], refs[-8:-6], refs[-4:-2]
-    outs, (packed, sem) = refs[-6:-4], refs[-2:]
-    k = pl.program_id(0)
-    feat = ins[0].shape[-1]
+    )(column, meta, *[f_in] * wide, *l_in)
+
+
+def finish_kernel(column, meta, *refs):
+    first, last, sums, outs = (refs[n : n + 4] for n in range(0, 16, 4))
+    ways, (packed, sem) = refs[16:18], refs[18:]
+    kind, k = pl.program_id(0), pl.program_id(1)
+    feat = last[0].shape[-1]
     spare = meta[0] != 0
     foreign = spare | ((meta[1] != 0) & (k == 1))
-    each = 3 if symmetric else 4
-    for kind in range(2):
-        f = ins[-1][:, kind, 0].reshape(-1, feat)
-        l = ins[0][:, kind, 0].reshape(-1, feat)
-        total = sums[kind][0] + dot_rows(l, f)
-        outs[kind][0] = jnp.where(foreign, 0.0, total)
-
-        @pl.when(foreign)
+    f = jnp.concatenate([ref[0, 0, 0] for ref in first], axis=0)
+    l = jnp.concatenate([ref[0, 0, 0] for ref in last], axis=0)
+    both = dot_rows(jnp.concatenate([f, l], axis=1), f)
+
+    def copies(way, which):
+        return [
+            pltpu.make_async_copy(
+                packed.at[way, pl.ds(start, count)], ways[way].at[pl.ds(start, count)], sem.at[way, which, part]
+            )
+            for part, (start, count) in enumerate([(5 * which, 5), (10 + 8 * which, 8)])
+        ]
+
+    for which in range(2):
+
+        @pl.when(kind == which)
         def _():
-            pieces = corners(total, symmetric)
+            factor = sums[2 * which][0] + both[:feat]
+            between = sums[2 * which + 1][0] + both[feat:]
+            outs[2 * which][0] = jnp.where(foreign, 0.0, factor)
+            outs[2 * which + 1][0] = jnp.where(foreign, 0.0, between)
             for way, chosen in ((0, spare == (k == 0)), (1, k == 1)):
 
-                @pl.when(chosen)
+                @pl.when(foreign & chosen)
                 def _():
-                    for n, piece in enumerate(pieces):
-                        packed[way, each * kind + n] = piece
-
-    @pl.when(foreign & (k == 1))
+                    for n, piece in enumerate(pack_symmetric(factor)):
+                        packed[way, 5 * which + n] = piece.astype(jnp.bfloat16)
+                    for n, piece in enumerate(pack_whole(between)):
+                        packed[way, 10 + 8 * which + n] = piece.astype(jnp.bfloat16)
+                    for copy in copies(way, which):
+                        copy.start()
+
+    @pl.when(foreign & (k == 1) & (kind == 1))
     def _():
-        copies = [
-            pltpu.make_async_copy(packed.at[way], ways[way].at[pl.ds(base, 2 * each)], sem.at[way])
-            for way in range(2)
-        ]
-        for copy in copies:
-            copy.start()
-        for copy in copies:
-            copy.wait()
-
-
-def finish(meta, f_swap, l_in, sums, ways):
-    symmetric = l_in is None
-    ins = [f_swap] if symmetric else [l_in, f_swap]
+        for way in range(2):
+            for which in range(2):
+                for copy in copies(way, which):
+                    copy.wait()
+
+
+def finish(column, meta, f_swap, l_in, sums):
     wide, _, _, rows, feat = f_swap.shape
-    each, base = (3, 0) if symmetric else (4, 6)
-    way = jax.ShapeDtypeStruct((14, feat // 2, feat // 2), jnp.bfloat16)
+    one = (1, 1, 1, rows, feat)
+    here = lambda kind, k, c, m: (kind, k)
+    own = [
+        pl.BlockSpec((1, feat, feat), lambda kind, k, c, m: (jnp.where(kind == 0, k, KEEP - 1), 0, 0)),
+        pl.BlockSpec((1, feat, feat), lambda kind, k, c, m: (jnp.where(kind == 1, k, 0), 0, 0)),
+    ]
+    blocks = [own[0], own[0], own[1], own[1]]
+    way = jax.ShapeDtypeStruct((26, feat // 4, feat // 2), jnp.bfloat16)
     out = jax.ShapeDtypeStruct((2 * KEEP, feat, feat), jnp.float32)
-    block = pl.BlockSpec((1, feat, feat), lambda k, m: (k, 0, 0))
     anywhere = pl.BlockSpec(memory_space=pl.ANY)
-    aliases = {1 + len(ins) + len(ways) + n: n for n in range(2)}
-    aliases.update({1 + len(ins) + n: 2 + n for n in range(len(ways))})
     return pl.pallas_call(
-        functools.partial(finish_kernel, symmetric, base),
+        finish_kernel,
         grid_spec=pltpu.PrefetchScalarGridSpec(
-            num_scalar_prefetch=1,
-            grid=(KEEP,),
-            in_specs=[pl.BlockSpec((wide, 2, 1, rows, feat), lambda k, m: (0, 0, k, 0, 0))] * len(ins)
-            + [anywhere] * len(ways)
-            + [block] * 2,
-            out_specs=[block] * 2 + [anywhere] * 2,
+            num_scalar_prefetch=2,
+            grid=(2, KEEP),
+            in_specs=[pl.BlockSpec(one, index) for index in by_sender(f_swap.shape, here)]
+            + [pl.BlockSpec(one, lambda kind, k, c, m: (0, kind, k, 0, 0))] * wide
+            + blocks,
+            out_specs=blocks + [anywhere] * 2,
             scratch_shapes=[
-                pltpu.VMEM((2, 2 * each, feat // 2, feat // 2), jnp.bfloat16),
-                pltpu.SemaphoreType.DMA((2,)),
+                pltpu.VMEM((2,) + way.shape, jnp.bfloat16),
+                pltpu.SemaphoreType.DMA((2, 2, 2)),
             ],
         ),
-        out_shape=[out, out, way, way],
-        input_output_aliases=aliases,
-        compiler_params=pltpu.CompilerParams(vmem_limit_bytes=60 << 20),
+        out_shape=[out] * 4 + [way] * 2,
+        input_output_aliases={2 + 2 * wide + n: n for n in range(4)},
+        compiler_params=pltpu.CompilerParams(vmem_limit_bytes=32 << 20),
         name="finish",
-    )(meta, *ins, *ways, *sums)
+    )(column, meta, *[f_swap] * wide, *l_in, *sums)
 
 
 def fill_kernel(meta, *refs):
     ways, outs, (half, wide, load_sem, store_sem) = refs[:2], refs[6:10], refs[10:]
     feat = wide.shape[-1]
-    h = feat // 2
+    h = feat // 4
     slots = [meta[2], meta[3]]
     loads = [pltpu.make_async_copy(ways[w], half.at[w], load_sem.at[w]) for w in range(2)]
 
@@ -288,16 +320,17 @@
             loads[w].wait()
             started = stores(w)
             for kind in range(2):
-                for n, (i, j) in enumerate([(0, 0), (0, 1), (1, 1)]):
-                    piece = half[w, 3 * kind + n].astype(jnp.float32)
-                    wide[w, 2 * kind, i * h : i * h + h, j * h : j * h + h] = piece
-                    if i != j:
-                        wide[w, 2 * kind, j * h : j * h + h, i * h : i * h + h] = piece.T
+                for n, pair in enumerate(symmetric_tiles(feat)):
+                    for m, (i, j) in enumerate(pair):
+                        piece = half[w, 5 * kind + n, :, m * h : m * h + h].astype(jnp.float32)
+                        wide[w, 2 * kind, i * h : i * h + h, j * h : j * h + h] = piece
+                        if i != j:
+                            wide[w, 2 * kind, j * h : j * h + h, i * h : i * h + h] = piece.T
                 started[2 * kind].start()
-                for n in range(4):
+                for n in range(8):
                     i, j = n // 2, n % 2
-                    piece = half[w, 6 + 4 * kind + n].astype(jnp.float32)
-                    wide[w, 2 * kind + 1, i * h : i * h + h, j * h : j * h + h] = piece
+                    piece = half[w, 10 + 8 * kind + n].astype(jnp.float32)
+                    wide[w, 2 * kind + 1, i * h : i * h + h, 2 * j * h : 2 * j * h + 2 * h] = piece
                 started[2 * kind + 1].start()
 
     for w in range(2):
@@ -345,7 +378,8 @@
     groups = lax.axis_size("dp")
     sections = lax.axis_size("section")
     table = jnp.asarray(plan_table(groups))
-    f, meta = prepare(doc_lengths, block_owner, table, first_acts[0], first_grads[0], groups, False)
+    column = (lax.axis_index("dp") // 2).astype(jnp.int32).reshape(1)
+    f_own, f_other, meta = prepare(doc_lengths, block_owner, table, first_acts[0], first_grads[0], groups, False)
     meta, last_acts, last_grads = lax.optimization_barrier((meta, last_acts, last_grads))
     l_own, l_other, _ = prepare(doc_lengths, block_owner, table, last_acts[0], last_grads[0], groups, True)
 
@@ -357,17 +391,20 @@
     def exchange(x):
         return lax.all_to_all(x, "dp", split_axis=0, concat_axis=0, tiled=True, axis_index_groups=rows_of)
 
+    def spread(x):
+        turns = [[(i, i // groups * groups + (i + 2 * n) % groups) for i in range(sections * groups)] for n in range(4)]
+        return [x] + [lax.ppermute(x[n : n + 1], AXES, turns[n]) for n in range(1, 4)]
+
     l_own = lax.ppermute(l_own, AXES, straight)
     l_other = lax.ppermute(l_other, AXES, across)
-    f_in = exchange(f)
-    f_in, l_own = lax.optimization_barrier((f_in, l_own))
-    f_swap = lax.ppermute(f_in[:, 1], AXES, swap)
-    l_own = exchange(l_own)
-    l_own, l_other = lax.optimization_barrier((l_own, l_other))
-    l_other = exchange(l_other)
-    af, ac, gf, gc = begin(f_in, l_own)
-    af, gf, *ways = finish(meta, f_swap, None, (af, gf), ())
-    ac, gc, *ways = finish(meta, f_swap, l_other, (ac, gc), ways)
+    f_other = exchange(f_other)
+    f_other, f_own = lax.optimization_barrier((f_other, f_own))
+    f_swap = lax.ppermute(f_other, AXES, swap)
+    f_own = exchange(f_own)
+    l_own = spread(l_own)
+    l_other = spread(l_other)
+    sums = begin(column, meta, f_own, l_own)
+    af, ac, gf, gc, *ways = finish(column, meta, f_swap, l_other, sums)
     got = hand_over(meta[4], groups, *ways)
     af, ac, gf, gc = fill(meta, *got, (af, ac, gf, gc))
     return af[None, None], gf[None, None], ac[None, None], gc[None, None]

time: 200 us -> 184 us (0.920); the launches traced: 200 us -> 182 us
  waiting for transfers between devices: 124 us -> 109 us
  Pallas kernels: 38.4 us -> 34.8 us
  starting transfers between devices: 29.2 us -> 26.9 us
    ppermute x1, waiting for transfers between devices: 47 us -> 22.9 us  [on_device(): l_own = lax.ppermute(l_own, AXES, straight)]
    ppermute x1 -> x7, starting transfers between devices: 0.01 us -> 7.08 us  [the longest x6 5.85 us: spread(): return [x] + [lax.ppermute(x[n:n + 1], AXES, turns[n]) for n in range(1, 4)]]
    ppermute x1 -> x7, waiting for transfers between devices: 0.01 us -> 6.32 us  [the longest x6 6.31 us: spread(): return [x] + [lax.ppermute(x[n:n + 1], AXES, turns[n]) for n in range(1, 4)]]
    all_to_all x3 -> x2, waiting for transfers between devices: 6.88 us -> 12.8 us  [exchange(): lax.all_to_all(x, 'dp', split_axis=0, concat_axis=0, tiled=True, axis_ind...]
    ppermute x2, starting transfers between devices: 7.63 us -> 2.63 us  [along(): sent.append(lax.ppermute(value, AXES, pairs))]
    slice x0 -> x2, local copies, waits for them, and re-layouts: none -> 4.81 us  [spread(): return [x] + [lax.ppermute(x[n:n + 1], AXES, turns[n]) for n in range(1, 4)]]
    all_to_all x3 -> x2, starting transfers between devices: 14.9 us -> 10.5 us  [exchange(): lax.all_to_all(x, 'dp', split_axis=0, concat_axis=0, tiled=True, axis_ind...]
    pallas_call x5 -> x4, Pallas kernels: 34 us -> 30.4 us  [the longest x1 11.3 us: finish(): pl.pallas_call(finish_kernel, grid_spec=pltpu.PrefetchScalarGridSpec(num_...]
  transfers between devices with their start and end apart: 8 -> 13, of which waited for: 5 -> 6; matrix products, arithmetic and copies ran while one was open for 2% -> 3% of each run, Pallas kernels for 10% -> 8%
where the time goes in v1:
time: 184 us; the launch traced here: 182 us
  waiting for transfers between devices  109 us (59%)
  Pallas kernels  34.8 us (19%)
  starting transfers between devices  26.9 us (15%)
  local copies, waits for them, and re-layouts  9.14 us (5%)
    ppermute x1, waiting for transfers between devices, on_device(): l_other = lax.ppermute(l_other, AXES, across)  45.8 us
    ppermute x1, waiting for transfers between devices, on_device(): l_own = lax.ppermute(l_own, AXES, straight)  22.9 us
    ppermute x2, waiting for transfers between devices, along(): sent.append(lax.ppermute(value, AXES, pairs))  21.5 us
    all_to_all x2, waiting for transfers between devices, exchange(): lax.all_to_all(x, 'dp', split_axis=0, concat_axis=0, tiled=True, axis_ind...  12.8 us
    pallas_call x1, Pallas kernels, finish(): pl.pallas_call(finish_kernel, grid_spec=pltpu.PrefetchScalarGridSpec(num_...  11.3 us
    all_to_all x2, starting transfers between devices, exchange(): lax.all_to_all(x, 'dp', split_axis=0, concat_axis=0, tiled=True, axis_ind...  10.5 us
    pallas_call x2, Pallas kernels, prepare(): pl.pallas_call(functools.partial(prepare_kernel, groups, relative), grid=...  10.3 us
    pallas_call x1, Pallas kernels, begin(): pl.pallas_call(begin_kernel, grid_spec=pltpu.PrefetchScalarGridSpec(num_s...  8.83 us
  transfers between devices with their start and end apart: 13, of which 6 were waited for; matrix products, arithmetic and copies ran while one was open for 3% of the time, Pallas kernels for 8%

profile of v1, /device:TPU:30, one launch (start us, length us, event | category | flops | bytes accessed | tf_op | source)
XLA Modules:
  0.0 181.6 jit_solution(3410619334474682556)
XLA Ops:
  0.6 5.2 %prepare.2 = (bf16[4,2,2,128,512]{4,3,2,1,0:T(8,128)(2,1)}, bf16[4,2,2,128,512]{4,3,2,1,0:T(8,128)(2,1)}, s32[8]{0:T(128)}) custom-call(s32[1,16]{1,0:T(1,128)} %lengths.3, s32[16]{0:T(128)} %owner.3, s32[1024]{0:T(1024)} %constant.26.clone.table, bf16[128,8192]{1,0:T(8,128)(2,1)} %bitcast.14, bf16[128,8192]{1,0:T(8,128)(2,1)} %bitcast.15), custom_call_target="tpu_custom_call" | custom-call | tf_op jit(solution)/shard_map/prepare/pallas_call | solution.py:129
  5.8 4.9 %all-to-all-start = ((bf16[4,2,2,128,512]{4,3,2,1,0:T(8,128)(2,1)}), bf16[4,2,2,128,512]{4,3,2,1,0:T(8,128)(2,1)}, u32[]{:S(2)}, u32[]{:S(2)}) async-start(bf16[4,2,2,128,512]{4,3,2,1,0:T(8,128)(2,1)} %get-tuple-element.86), calls=%async_computation | async-start | bytes 4194304 | tf_op jit(solution)/shard_map/all_to_all | solution.py:392
  10.7 5.1 %prepare.3 = (bf16[4,2,2,128,512]{4,3,2,1,0:T(8,128)(2,1)}, bf16[4,2,2,128,512]{4,3,2,1,0:T(8,128)(2,1)}, s32[8]{0:T(128)}) custom-call(s32[1,16]{1,0:T(1,128)} %lengths.3, s32[16]{0:T(128)} %owner.3, s32[1024]{0:T(1024)} %constant.26.clone.table, bf16[128,8192]{1,0:T(8,128)(2,1)} %bitcast.16, bf16[128,8192]{1,0:T(8,128)(2,1)} %bitcast.17), custom_call_target="tpu_custom_call" | custom-call | tf_op jit(solution)/shard_map/prepare/pallas_call | solution.py:129
  15.8 1.9 %collective-permute-start.23 = (bf16[4,2,2,128,512]{4,3,2,1,0:T(8,128)(2,1)}, bf16[4,2,2,128,512]{4,3,2,1,0:T(8,128)(2,1)}, u32[]{:S(2)}, u32[]{:S(2)}) collective-permute-start(bf16[4,2,2,128,512]{4,3,2,1,0:T(8,128)(2,1)} %get-tuple-element.93), channel_id=1, source_target_pairs={{0,8},{1,9},{2,10},{3,11},{4,12},{5,13},{6,14},{7,15},{8,16},{9,17... | collective-permute-start | bytes 6291464 | tf_op jit(solution)/shard_map/ppermute | solution.py:398
  17.7 4.8 %collective-permute-start.19 = (bf16[4,2,2,128,512]{4,3,2,1,0:T(8,128)(2,1)}, bf16[4,2,2,128,512]{4,3,2,1,0:T(8,128)(2,1)}, u32[]{:S(2)}, u32[]{:S(2)}) collective-permute-start(bf16[4,2,2,128,512]{4,3,2,1,0:T(8,128)(2,1)} %get-tuple-element.91), channel_id=1, source_target_pairs={{0,9},{1,8},{2,11},{3,10},{4,13},{5,12},{6,15},{7,14},{8,17},{9,16... | collective-permute-start | bytes 6291464 | tf_op jit(solution)/shard_map/ppermute | solution.py:399
  22.5 12.8 %all-to-all-done = bf16[4,2,2,128,512]{4,3,2,1,0:T(8,128)(2,1)} async-done(((bf16[4,2,2,128,512]{4,3,2,1,0:T(8,128)(2,1)}), bf16[4,2,2,128,512]{4,3,2,1,0:T(8,128)(2,1)}, u32[]{:S(2)}, u32[]{:S(2)}) %all-to-all-start) | async-done | bytes 2097184 | tf_op jit(solution)/shard_map/all_to_all | solution.py:392
  35.3 1.2 collective-permute-start.18
  36.6 5.7 %all-to-all-start.1 = ((bf16[4,2,2,128,512]{4,3,2,1,0:T(8,128)(2,1)}), bf16[4,2,2,128,512]{4,3,2,1,0:T(8,128)(2,1)S(1)}, u32[]{:S(2)}, u32[]{:S(2)}) async-start(bf16[4,2,2,128,512]{4,3,2,1,0:T(8,128)(2,1)} %get-tuple-element.92), calls=%async_computation.1 | async-start | bytes 4194304 | tf_op jit(solution)/shard_map/all_to_all | solution.py:392
  42.2 22.9 %collective-permute-done.23.refs_4_ = bf16[4,2,2,128,512]{4,3,2,1,0:T(8,128)(2,1)} collective-permute-done((bf16[4,2,2,128,512]{4,3,2,1,0:T(8,128)(2,1)}, bf16[4,2,2,128,512]{4,3,2,1,0:T(8,128)(2,1)}, u32[]{:S(2)}, u32[]{:S(2)}) %collective-permute-start.23) | collective-permute-done | bytes 2097184 | tf_op jit(solution)/shard_map/ppermute | solution.py:398
  65.1 2.3 %fusion = (bf16[1,2,2,128,512]{4,3,2,1,0:T(8,128)(2,1)}, bf16[1,2,2,128,512]{4,3,2,1,0:T(8,128)(2,1)S(1)}, bf16[1,2,2,128,512]{4,3,2,1,0:T(8,128)(2,1)S(1)}) fusion(bf16[4,2,2,128,512]{4,3,2,1,0:T(8,128)(2,1)} %collective-permute-done.23.refs_4_), kind=kLoop, calls=%fused_computation | loop fusion | bytes 3145728 | tf_op jit(solution)/shard_map/slice | solution.py:396
  67.5 2.8 %collective-permute-start.25 = (bf16[1,2,2,128,512]{4,3,2,1,0:T(8,128)(2,1)S(1)}, bf16[1,2,2,128,512]{4,3,2,1,0:T(8,128)(2,1)S(1)}, u32[]{:S(2)}, u32[]{:S(2)}) collective-permute-start(bf16[1,2,2,128,512]{4,3,2,1,0:T(8,128)(2,1)S(1)} %get-tuple-element.111), channel_id=1, source_target_pairs={{0,4},{1,5},{2,6},{3,7},{4,0},{5,1},{6,2},{7,3},{8,12},{9,13},{10,... | collective-permute-start | bytes 1572872 | tf_op jit(solution)/shard_map/ppermute | solution.py:396
  70.3 45.8 %collective-permute-done.19.refs_4_ = bf16[4,2,2,128,512]{4,3,2,1,0:T(8,128)(2,1)} collective-permute-done((bf16[4,2,2,128,512]{4,3,2,1,0:T(8,128)(2,1)}, bf16[4,2,2,128,512]{4,3,2,1,0:T(8,128)(2,1)}, u32[]{:S(2)}, u32[]{:S(2)}) %collective-permute-start.19) | collective-permute-done | bytes 2097184 | tf_op jit(solution)/shard_map/ppermute | solution.py:399
  116.1 2.6 %fusion.1 = (bf16[1,2,2,128,512]{4,3,2,1,0:T(8,128)(2,1)}, bf16[1,2,2,128,512]{4,3,2,1,0:T(8,128)(2,1)}, bf16[1,2,2,128,512]{4,3,2,1,0:T(8,128)(2,1)}) fusion(bf16[4,2,2,128,512]{4,3,2,1,0:T(8,128)(2,1)} %collective-permute-done.19.refs_4_), kind=kLoop, calls=%fused_computation.1 | loop fusion | bytes 3145728 | tf_op jit(solution)/shard_map/slice | solution.py:396
  119.5 2.8 %collective-permute-start.21 = (bf16[1,2,2,128,512]{4,3,2,1,0:T(8,128)(2,1)}, bf16[1,2,2,128,512]{4,3,2,1,0:T(8,128)(2,1)S(1)}, u32[]{:S(2)}, u32[]{:S(2)}) collective-permute-start(bf16[1,2,2,128,512]{4,3,2,1,0:T(8,128)(2,1)} %get-tuple-element.114), channel_id=1, source_target_pairs={{0,4},{1,5},{2,6},{3,7},{4,0},{5,1},{6,2},{7,3},{8,12},{9,13},{10,... | collective-permute-start | bytes 1572872 | tf_op jit(solution)/shard_map/ppermute | solution.py:396
  124.6 1.0 copy-done.1
  125.6 1.0 copy-done.3
  126.7 8.8 %begin.1 = (f32[4,512,512]{2,1,0:T(8,128)}, f32[4,512,512]{2,1,0:T(8,128)}, f32[4,512,512]{2,1,0:T(8,128)}, f32[4,512,512]{2,1,0:T(8,128)}) custom-call(s32[1]{0:T(128)} %bitcast.3.column, s32[8]{0:T(128)S(1)} %copy-done.4, bf16[4,2,2,128,512]{4,3,2,1,0:T(8,128)(2,1)S(1)} %all-to-all-done.1.refs_0_.refs_1_.refs_2_.refs_3_, ...), custom_call_target="tpu_custom_call" | custom-call | tf_op jit(solution)/shard_map/begin/pallas_call | solution.py:204
  135.5 6.3 %collective-permute-done.22.refs_7_ = bf16[1,2,2,128,512]{4,3,2,1,0:T(8,128)(2,1)} collective-permute-done((bf16[1,2,2,128,512]{4,3,2,1,0:T(8,128)(2,1)}, bf16[1,2,2,128,512]{4,3,2,1,0:T(8,128)(2,1)}, u32[]{:S(2)}, u32[]{:S(2)}) %collective-permute-start.22) | collective-permute-done | bytes 524320 | tf_op jit(solution)/shard_map/ppermute | solution.py:396
  141.8 11.3 %finish.1 = (f32[4,512,512]{2,1,0:T(8,128)}, f32[4,512,512]{2,1,0:T(8,128)}, f32[4,512,512]{2,1,0:T(8,128)}, f32[4,512,512]{2,1,0:T(8,128)}, bf16[26,128,256]{2,...) custom-call(s32[1]{0:T(128)} %bitcast.3.column, ...), custom_call_target="tpu_custom_call", output_to_operand_aliasing={{0}: (10, {}), {1}: (11, {}), {2}: (12, {}), {3}: (13, {})} | custom-call | tf_op jit(solution)/shard_map/finish/pallas_call | solution.py:277
  153.1 24.1 %conditional.1 = (bf16[26,128,256]{2,1,0:T(8,128)(2,1)}, bf16[26,128,256]{2,1,0:T(8,128)(2,1)}) conditional(s32[]{:T(128)} %bitcast.2, (bf16[26,128,256]{2,1,0:T(8,128)(2,1)S(1)}, bf16[26,128,256]{2,1,0:T(8,128)(2,1)S(1)}) %tuple.48, (bf16[26,128,256]{2,1,0:T(8,128)(2,1)S(1)}, ...), branch_computations={%region_0.1_spmd, %region_1.2_spmd, %region_2.3_spmd, %region_3.4_... | conditional | bytes 13631584 | solution.py:374
  154.1 1.6 collective-permute-start.1
  155.7 19.8 %collective-permute-done = bf16[26,128,256]{2,1,0:T(8,128)(2,1)} collective-permute-done((bf16[26,128,256]{2,1,0:T(8,128)(2,1)S(1)}, bf16[26,128,256]{2,1,0:T(8,128)(2,1)}, u32[]{:S(2)}, u32[]{:S(2)}) %collective-permute-start) | collective-permute-done | bytes 1703968 | tf_op jit(solution)/shard_map/cond/branch_0_fun/ppermute | solution.py:371
  175.6 1.7 collective-permute-done.1
  177.2 4.4 %fill_slots.1 = (f32[4,512,512]{2,1,0:T(8,128)}, f32[4,512,512]{2,1,0:T(8,128)}, f32[4,512,512]{2,1,0:T(8,128)}, f32[4,512,512]{2,1,0:T(8,128)}) custom-call(s32[8]{0:T(128)} %get-tuple-element.85.meta, bf16[26,128,256]{2,1,0:T(8,128)(2,1)} %get-tuple-element.100.refs_0_, ...), custom_call_target="tpu_custom_call", output_to_operand_aliasing={{0}: (3, {}), {1}: (4, {}), {2}: (5, {}), {3}: (6, {})} | custom-call | tf_op jit(solution)/shard_map/fill_slots/pallas_call | solution.py:347
  (21 shorter events, 3.4 us)
Async XLA Ops:
  5.8 29.5 %all-to-all-start = ((bf16[4,2,2,128,512]{4,3,2,1,0:T(8,128)(2,1)}), bf16[4,2,2,128,512]{4,3,2,1,0:T(8,128)(2,1)}, u32[]{:S(2)}, u32[]{:S(2)}) async-start(bf16[4,2,2,128,512]{4,3,2,1,0:T(8,128)(2,1)} %get-tuple-element.86), calls=%async_computation | async-start | bytes 4194304 | tf_op jit(solution)/shard_map/all_to_all | solution.py:392
  15.8 49.3 %collective-permute-start.23 = (bf16[4,2,2,128,512]{4,3,2,1,0:T(8,128)(2,1)}, bf16[4,2,2,128,512]{4,3,2,1,0:T(8,128)(2,1)}, u32[]{:S(2)}, u32[]{:S(2)}) collective-permute-start(bf16[4,2,2,128,512]{4,3,2,1,0:T(8,128)(2,1)} %get-tuple-element.93), channel_id=1, source_target_pairs={{0,8},{1,9},{2,10},{3,11},{4,12},{5,13},{6,14},{7,15},{8,16},{9,17... | collective-permute-start | bytes 6291464 | tf_op jit(solution)/shard_map/ppermute | solution.py:398
  17.7 98.4 %collective-permute-start.19 = (bf16[4,2,2,128,512]{4,3,2,1,0:T(8,128)(2,1)}, bf16[4,2,2,128,512]{4,3,2,1,0:T(8,128)(2,1)}, u32[]{:S(2)}, u32[]{:S(2)}) collective-permute-start(bf16[4,2,2,128,512]{4,3,2,1,0:T(8,128)(2,1)} %get-tuple-element.91), channel_id=1, source_target_pairs={{0,9},{1,8},{2,11},{3,10},{4,13},{5,12},{6,15},{7,14},{8,17},{9,16... | collective-permute-start | bytes 6291464 | tf_op jit(solution)/shard_map/ppermute | solution.py:399
  35.3 106.5 %collective-permute-start.18 = (bf16[4,2,2,128,512]{4,3,2,1,0:T(8,128)(2,1)}, bf16[4,2,2,128,512]{4,3,2,1,0:T(8,128)(2,1)}, u32[]{:S(2)}, u32[]{:S(2)}) collective-permute-start(bf16[4,2,2,128,512]{4,3,2,1,0:T(8,128)(2,1)} %all-to-all-done), channel_id=1, source_target_pairs={{0,1},{1,0},{2,3},{3,2},{4,5},{5,4},{6,7},{7,6},{8,9},{9,8},{10,11... | collective-permute-start | bytes 6291464 | tf_op jit(solution)/shard_map/ppermute | solution.py:402
  36.6 88.0 %all-to-all-start.1 = ((bf16[4,2,2,128,512]{4,3,2,1,0:T(8,128)(2,1)}), bf16[4,2,2,128,512]{4,3,2,1,0:T(8,128)(2,1)S(1)}, u32[]{:S(2)}, u32[]{:S(2)}) async-start(bf16[4,2,2,128,512]{4,3,2,1,0:T(8,128)(2,1)} %get-tuple-element.92), calls=%async_computation.1 | async-start | bytes 4194304 | tf_op jit(solution)/shard_map/all_to_all | solution.py:392
  67.4 55.8 %copy-start.4 = (s32[8]{0:T(128)S(1)}, s32[8]{0:T(128)}, u32[]{:S(2)}) copy-start(s32[8]{0:T(128)} %get-tuple-element.85.meta) | copy-start | bytes 100
  67.4 51.4 %collective-permute-start.24 = (bf16[1,2,2,128,512]{4,3,2,1,0:T(8,128)(2,1)S(1)}, bf16[1,2,2,128,512]{4,3,2,1,0:T(8,128)(2,1)S(1)}, u32[]{:S(2)}, u32[]{:S(2)}) collective-permute-start(bf16[1,2,2,128,512]{4,3,2,1,0:T(8,128)(2,1)S(1)} %get-tuple-element.112), channel_id=1, source_target_pairs={{0,2},{1,3},{2,4},{3,5},{4,6},{5,7},{6,0},{7,1},{8,10},{9,11},{10,... | collective-permute-start | bytes 1572872 | tf_op jit(solution)/shard_map/ppermute | solution.py:396
  67.5 54.9 %collective-permute-start.25 = (bf16[1,2,2,128,512]{4,3,2,1,0:T(8,128)(2,1)S(1)}, bf16[1,2,2,128,512]{4,3,2,1,0:T(8,128)(2,1)S(1)}, u32[]{:S(2)}, u32[]{:S(2)}) collective-permute-start(bf16[1,2,2,128,512]{4,3,2,1,0:T(8,128)(2,1)S(1)} %get-tuple-element.111), channel_id=1, source_target_pairs={{0,4},{1,5},{2,6},{3,7},{4,0},{5,1},{6,2},{7,3},{8,12},{9,13},{10,... | collective-permute-start | bytes 1572872 | tf_op jit(solution)/shard_map/ppermute | solution.py:396
  70.3 54.3 %collective-permute-start.26 = (bf16[1,2,2,128,512]{4,3,2,1,0:T(8,128)(2,1)}, bf16[1,2,2,128,512]{4,3,2,1,0:T(8,128)(2,1)}, u32[]{:S(2)}, u32[]{:S(2)}) collective-permute-start(bf16[1,2,2,128,512]{4,3,2,1,0:T(8,128)(2,1)} %get-tuple-element.110), channel_id=1, source_target_pairs={{0,6},{1,7},{2,0},{3,1},{4,2},{5,3},{6,4},{7,5},{8,14},{9,15},{10,... | collective-permute-start | bytes 1572872 | tf_op jit(solution)/shard_map/ppermute | solution.py:396
  118.7 16.8 %collective-permute-start.20 = (bf16[1,2,2,128,512]{4,3,2,1,0:T(8,128)(2,1)}, bf16[1,2,2,128,512]{4,3,2,1,0:T(8,128)(2,1)S(1)}, u32[]{:S(2)}, u32[]{:S(2)}) collective-permute-start(bf16[1,2,2,128,512]{4,3,2,1,0:T(8,128)(2,1)} %get-tuple-element.115), channel_id=1, source_target_pairs={{0,2},{1,3},{2,4},{3,5},{4,6},{5,7},{6,0},{7,1},{8,10},{9,11},{10,... | collective-permute-start | bytes 1572872 | tf_op jit(solution)/shard_map/ppermute | solution.py:396
  118.8 0.8 copy-start
  119.5 16.0 %collective-permute-start.21 = (bf16[1,2,2,128,512]{4,3,2,1,0:T(8,128)(2,1)}, bf16[1,2,2,128,512]{4,3,2,1,0:T(8,128)(2,1)S(1)}, u32[]{:S(2)}, u32[]{:S(2)}) collective-permute-start(bf16[1,2,2,128,512]{4,3,2,1,0:T(8,128)(2,1)} %get-tuple-element.114), channel_id=1, source_target_pairs={{0,4},{1,5},{2,6},{3,7},{4,0},{5,1},{6,2},{7,3},{8,12},{9,13},{10,... | collective-permute-start | bytes 1572872 | tf_op jit(solution)/shard_map/ppermute | solution.py:396
  122.4 0.8 copy-start.2
  123.2 18.6 %collective-permute-start.22 = (bf16[1,2,2,128,512]{4,3,2,1,0:T(8,128)(2,1)}, bf16[1,2,2,128,512]{4,3,2,1,0:T(8,128)(2,1)}, u32[]{:S(2)}, u32[]{:S(2)}) collective-permute-start(bf16[1,2,2,128,512]{4,3,2,1,0:T(8,128)(2,1)} %get-tuple-element.113), channel_id=1, source_target_pairs={{0,6},{1,7},{2,0},{3,1},{4,2},{5,3},{6,4},{7,5},{8,14},{9,15},{10,... | collective-permute-start | bytes 1572872 | tf_op jit(solution)/shard_map/ppermute | solution.py:396
  124.6 1.0 copy-start.1
  125.6 1.0 copy-start.3
  153.1 22.5 %collective-permute-start = (bf16[26,128,256]{2,1,0:T(8,128)(2,1)S(1)}, bf16[26,128,256]{2,1,0:T(8,128)(2,1)}, u32[]{:S(2)}, u32[]{:S(2)}) collective-permute-start(bf16[26,128,256]{2,1,0:T(8,128)(2,1)S(1)} %get-tuple-element.36), channel_id=1, source_target_pairs={{0,2},{1,3},{2,4},{3,5},{4,6},{5,7},{6,0},{7,1},{8,10},{9,11},{10,... | collective-permute-start | bytes 5111816 | tf_op jit(solution)/shard_map/cond/branch_0_fun/ppermute | solution.py:371
  154.1 23.1 %collective-permute-start.1 = (bf16[26,128,256]{2,1,0:T(8,128)(2,1)S(1)}, bf16[26,128,256]{2,1,0:T(8,128)(2,1)}, u32[]{:S(2)}, u32[]{:S(2)}) collective-permute-start(bf16[26,128,256]{2,1,0:T(8,128)(2,1)S(1)} %get-tuple-element.37), channel_id=1, source_target_pairs={{0,6},{1,7},{2,0},{3,1},{4,2},{5,3},{6,4},{7,5},{8,14},{9,15},{10,... | collective-permute-start | bytes 5111816 | tf_op jit(solution)/shard_map/cond/branch_0_fun/ppermute | solution.py:371

commit v2 on v1

--- a/solution.py
+++ b/solution.py
@@ -116,7 +116,7 @@
 def prepare(lengths, owner, table, one, two, groups, relative):
     rows, width = one.shape
     feat = width // owner.shape[0]
-    cut = rows // 4
+    cut = rows // 2
     wide = groups // 2
     shapes = [(wide, 2, KEEP, rows, feat)] * 2
     smem = pl.BlockSpec(memory_space=pltpu.SMEM)

time: 184 us -> 182 us (0.989)
  starting transfers between devices: 26.9 us -> 30.4 us
  waiting for transfers between devices: 109 us -> 106 us
  Pallas kernels: 34.8 us -> 32.8 us
    ppermute x6, waiting for transfers between devices: 6.31 us -> 2.79 us  [spread(): return [x] + [lax.ppermute(x[n:n + 1], AXES, turns[n]) for n in range(1, 4)]]
    ppermute x2, starting transfers between devices: 2.63 us -> 6.09 us  [along(): sent.append(lax.ppermute(value, AXES, pairs))]
    pallas_call x2, Pallas kernels: 10.3 us -> 8.32 us  [prepare(): pl.pallas_call(functools.partial(prepare_kernel, groups, relative), grid=...]
  transfers between devices with their start and end apart: 13 -> 13, of which waited for: 6 -> 6; matrix products, arithmetic and copies ran while one was open for 3% -> 3% of each run, Pallas kernels for 8% -> 7%
where the time goes in v2:
time: 182 us; the launch traced here: 180 us
  waiting for transfers between devices  106 us (58%)
  Pallas kernels  32.8 us (18%)
  starting transfers between devices  30.4 us (17%)
  local copies, waits for them, and re-layouts  9.14 us (5%)
    ppermute x1, waiting for transfers between devices, on_device(): l_other = lax.ppermute(l_other, AXES, across)  45.8 us
    ppermute x1, waiting for transfers between devices, on_device(): l_own = lax.ppermute(l_own, AXES, straight)  21.9 us
    ppermute x2, waiting for transfers between devices, along(): sent.append(lax.ppermute(value, AXES, pairs))  21.8 us
    all_to_all x2, waiting for transfers between devices, exchange(): lax.all_to_all(x, 'dp', split_axis=0, concat_axis=0, tiled=True, axis_ind...  13.8 us
    pallas_call x1, Pallas kernels, finish(): pl.pallas_call(finish_kernel, grid_spec=pltpu.PrefetchScalarGridSpec(num_...  11.3 us
    all_to_all x2, starting transfers between devices, exchange(): lax.all_to_all(x, 'dp', split_axis=0, concat_axis=0, tiled=True, axis_ind...  10.5 us
    pallas_call x1, Pallas kernels, begin(): pl.pallas_call(begin_kernel, grid_spec=pltpu.PrefetchScalarGridSpec(num_s...  8.83 us
    pallas_call x2, Pallas kernels, prepare(): pl.pallas_call(functools.partial(prepare_kernel, groups, relative), grid=...  8.32 us
  transfers between devices with their start and end apart: 13, of which 6 were waited for; matrix products, arithmetic and copies ran while one was open for 3% of the time, Pallas kernels for 7%

profile of v2, /device:TPU:30, one launch (start us, length us, event | category | flops | bytes accessed | tf_op | source)
XLA Modules:
  0.0 179.9 jit_solution(8839301129762291947)
XLA Ops:
  0.6 4.2 %prepare.2 = (bf16[4,2,2,128,512]{4,3,2,1,0:T(8,128)(2,1)}, bf16[4,2,2,128,512]{4,3,2,1,0:T(8,128)(2,1)}, s32[8]{0:T(128)}) custom-call(s32[1,16]{1,0:T(1,128)} %lengths.3, s32[16]{0:T(128)} %owner.3, s32[1024]{0:T(1024)} %constant.26.clone.table, bf16[128,8192]{1,0:T(8,128)(2,1)} %bitcast.14, bf16[128,8192]{1,0:T(8,128)(2,1)} %bitcast.15), custom_call_target="tpu_custom_call" | custom-call | tf_op jit(solution)/shard_map/prepare/pallas_call | solution.py:129
  4.8 4.9 %all-to-all-start = ((bf16[4,2,2,128,512]{4,3,2,1,0:T(8,128)(2,1)}), bf16[4,2,2,128,512]{4,3,2,1,0:T(8,128)(2,1)}, u32[]{:S(2)}, u32[]{:S(2)}) async-start(bf16[4,2,2,128,512]{4,3,2,1,0:T(8,128)(2,1)} %get-tuple-element.86), calls=%async_computation | async-start | bytes 4194304 | tf_op jit(solution)/shard_map/all_to_all | solution.py:392
  9.7 4.1 %prepare.3 = (bf16[4,2,2,128,512]{4,3,2,1,0:T(8,128)(2,1)}, bf16[4,2,2,128,512]{4,3,2,1,0:T(8,128)(2,1)}, s32[8]{0:T(128)}) custom-call(s32[1,16]{1,0:T(1,128)} %lengths.3, s32[16]{0:T(128)} %owner.3, s32[1024]{0:T(1024)} %constant.26.clone.table, bf16[128,8192]{1,0:T(8,128)(2,1)} %bitcast.16, bf16[128,8192]{1,0:T(8,128)(2,1)} %bitcast.17), custom_call_target="tpu_custom_call" | custom-call | tf_op jit(solution)/shard_map/prepare/pallas_call | solution.py:129
  13.8 1.9 %collective-permute-start.23 = (bf16[4,2,2,128,512]{4,3,2,1,0:T(8,128)(2,1)}, bf16[4,2,2,128,512]{4,3,2,1,0:T(8,128)(2,1)}, u32[]{:S(2)}, u32[]{:S(2)}) collective-permute-start(bf16[4,2,2,128,512]{4,3,2,1,0:T(8,128)(2,1)} %get-tuple-element.93), channel_id=1, source_target_pairs={{0,8},{1,9},{2,10},{3,11},{4,12},{5,13},{6,14},{7,15},{8,16},{9,17... | collective-permute-start | bytes 6291464 | tf_op jit(solution)/shard_map/ppermute | solution.py:398
  15.8 4.8 %collective-permute-start.19 = (bf16[4,2,2,128,512]{4,3,2,1,0:T(8,128)(2,1)}, bf16[4,2,2,128,512]{4,3,2,1,0:T(8,128)(2,1)}, u32[]{:S(2)}, u32[]{:S(2)}) collective-permute-start(bf16[4,2,2,128,512]{4,3,2,1,0:T(8,128)(2,1)} %get-tuple-element.91), channel_id=1, source_target_pairs={{0,9},{1,8},{2,11},{3,10},{4,13},{5,12},{6,15},{7,14},{8,17},{9,16... | collective-permute-start | bytes 6291464 | tf_op jit(solution)/shard_map/ppermute | solution.py:399
  20.5 13.8 %all-to-all-done = bf16[4,2,2,128,512]{4,3,2,1,0:T(8,128)(2,1)} async-done(((bf16[4,2,2,128,512]{4,3,2,1,0:T(8,128)(2,1)}), bf16[4,2,2,128,512]{4,3,2,1,0:T(8,128)(2,1)}, u32[]{:S(2)}, u32[]{:S(2)}) %all-to-all-start) | async-done | bytes 2097184 | tf_op jit(solution)/shard_map/all_to_all | solution.py:392
  34.3 1.2 collective-permute-start.18
  35.6 5.7 %all-to-all-start.1 = ((bf16[4,2,2,128,512]{4,3,2,1,0:T(8,128)(2,1)}), bf16[4,2,2,128,512]{4,3,2,1,0:T(8,128)(2,1)S(1)}, u32[]{:S(2)}, u32[]{:S(2)}) async-start(bf16[4,2,2,128,512]{4,3,2,1,0:T(8,128)(2,1)} %get-tuple-element.92), calls=%async_computation.1 | async-start | bytes 4194304 | tf_op jit(solution)/shard_map/all_to_all | solution.py:392
  41.2 21.9 %collective-permute-done.23.refs_4_ = bf16[4,2,2,128,512]{4,3,2,1,0:T(8,128)(2,1)} collective-permute-done((bf16[4,2,2,128,512]{4,3,2,1,0:T(8,128)(2,1)}, bf16[4,2,2,128,512]{4,3,2,1,0:T(8,128)(2,1)}, u32[]{:S(2)}, u32[]{:S(2)}) %collective-permute-start.23) | collective-permute-done | bytes 2097184 | tf_op jit(solution)/shard_map/ppermute | solution.py:398
  63.2 2.3 %fusion = (bf16[1,2,2,128,512]{4,3,2,1,0:T(8,128)(2,1)}, bf16[1,2,2,128,512]{4,3,2,1,0:T(8,128)(2,1)S(1)}, bf16[1,2,2,128,512]{4,3,2,1,0:T(8,128)(2,1)S(1)}) fusion(bf16[4,2,2,128,512]{4,3,2,1,0:T(8,128)(2,1)} %collective-permute-done.23.refs_4_), kind=kLoop, calls=%fused_computation | loop fusion | bytes 3145728 | tf_op jit(solution)/shard_map/slice | solution.py:396
  65.5 2.8 %collective-permute-start.25 = (bf16[1,2,2,128,512]{4,3,2,1,0:T(8,128)(2,1)S(1)}, bf16[1,2,2,128,512]{4,3,2,1,0:T(8,128)(2,1)S(1)}, u32[]{:S(2)}, u32[]{:S(2)}) collective-permute-start(bf16[1,2,2,128,512]{4,3,2,1,0:T(8,128)(2,1)S(1)} %get-tuple-element.111), channel_id=1, source_target_pairs={{0,4},{1,5},{2,6},{3,7},{4,0},{5,1},{6,2},{7,3},{8,12},{9,13},{10,... | collective-permute-start | bytes 1572872 | tf_op jit(solution)/shard_map/ppermute | solution.py:396
  68.3 45.8 %collective-permute-done.19.refs_4_ = bf16[4,2,2,128,512]{4,3,2,1,0:T(8,128)(2,1)} collective-permute-done((bf16[4,2,2,128,512]{4,3,2,1,0:T(8,128)(2,1)}, bf16[4,2,2,128,512]{4,3,2,1,0:T(8,128)(2,1)}, u32[]{:S(2)}, u32[]{:S(2)}) %collective-permute-start.19) | collective-permute-done | bytes 2097184 | tf_op jit(solution)/shard_map/ppermute | solution.py:399
  114.2 2.6 %fusion.1 = (bf16[1,2,2,128,512]{4,3,2,1,0:T(8,128)(2,1)}, bf16[1,2,2,128,512]{4,3,2,1,0:T(8,128)(2,1)}, bf16[1,2,2,128,512]{4,3,2,1,0:T(8,128)(2,1)}) fusion(bf16[4,2,2,128,512]{4,3,2,1,0:T(8,128)(2,1)} %collective-permute-done.19.refs_4_), kind=kLoop, calls=%fused_computation.1 | loop fusion | bytes 3145728 | tf_op jit(solution)/shard_map/slice | solution.py:396
  117.6 2.8 %collective-permute-start.21 = (bf16[1,2,2,128,512]{4,3,2,1,0:T(8,128)(2,1)}, bf16[1,2,2,128,512]{4,3,2,1,0:T(8,128)(2,1)S(1)}, u32[]{:S(2)}, u32[]{:S(2)}) collective-permute-start(bf16[1,2,2,128,512]{4,3,2,1,0:T(8,128)(2,1)} %get-tuple-element.114), channel_id=1, source_target_pairs={{0,4},{1,5},{2,6},{3,7},{4,0},{5,1},{6,2},{7,3},{8,12},{9,13},{10,... | collective-permute-start | bytes 1572872 | tf_op jit(solution)/shard_map/ppermute | solution.py:396
  123.7 1.0 copy-done.3
  124.7 8.8 %begin.1 = (f32[4,512,512]{2,1,0:T(8,128)}, f32[4,512,512]{2,1,0:T(8,128)}, f32[4,512,512]{2,1,0:T(8,128)}, f32[4,512,512]{2,1,0:T(8,128)}) custom-call(s32[1]{0:T(128)} %bitcast.3.column, s32[8]{0:T(128)S(1)} %copy-done.4, bf16[4,2,2,128,512]{4,3,2,1,0:T(8,128)(2,1)S(1)} %all-to-all-done.1.refs_0_.refs_1_.refs_2_.refs_3_, ...), custom_call_target="tpu_custom_call" | custom-call | tf_op jit(solution)/shard_map/begin/pallas_call | solution.py:204
  133.5 2.8 %collective-permute-done.22.refs_7_ = bf16[1,2,2,128,512]{4,3,2,1,0:T(8,128)(2,1)} collective-permute-done((bf16[1,2,2,128,512]{4,3,2,1,0:T(8,128)(2,1)}, bf16[1,2,2,128,512]{4,3,2,1,0:T(8,128)(2,1)}, u32[]{:S(2)}, u32[]{:S(2)}) %collective-permute-start.22) | collective-permute-done | bytes 524320 | tf_op jit(solution)/shard_map/ppermute | solution.py:396
  136.3 11.3 %finish.1 = (f32[4,512,512]{2,1,0:T(8,128)}, f32[4,512,512]{2,1,0:T(8,128)}, f32[4,512,512]{2,1,0:T(8,128)}, f32[4,512,512]{2,1,0:T(8,128)}, bf16[26,128,256]{2,...) custom-call(s32[1]{0:T(128)} %bitcast.3.column, ...), custom_call_target="tpu_custom_call", output_to_operand_aliasing={{0}: (10, {}), {1}: (11, {}), {2}: (12, {}), {3}: (13, {})} | custom-call | tf_op jit(solution)/shard_map/finish/pallas_call | solution.py:277
  147.6 27.9 %conditional.1 = (bf16[26,128,256]{2,1,0:T(8,128)(2,1)}, bf16[26,128,256]{2,1,0:T(8,128)(2,1)}) conditional(s32[]{:T(128)} %bitcast.2, (bf16[26,128,256]{2,1,0:T(8,128)(2,1)S(1)}, bf16[26,128,256]{2,1,0:T(8,128)(2,1)S(1)}) %tuple.48, (bf16[26,128,256]{2,1,0:T(8,128)(2,1)S(1)}, ...), branch_computations={%region_0.1_spmd, %region_1.2_spmd, %region_2.3_spmd, %region_3.4_... | conditional | bytes 13631584 | solution.py:374
  147.6 2.9 %collective-permute-start.2 = (bf16[26,128,256]{2,1,0:T(8,128)(2,1)S(1)}, bf16[26,128,256]{2,1,0:T(8,128)(2,1)}, u32[]{:S(2)}, u32[]{:S(2)}) collective-permute-start(bf16[26,128,256]{2,1,0:T(8,128)(2,1)S(1)} %get-tuple-element.38), channel_id=1, source_target_pairs={{1,0},{3,5},{5,7},{7,1},{9,8},{11,13},{13,15},{15,9},{17,16},{19,2... | collective-permute-start | bytes 5111816 | tf_op jit(solution)/shard_map/cond/branch_1_fun/ppermute | solution.py:371
  150.5 3.2 %collective-permute-start.3 = (bf16[26,128,256]{2,1,0:T(8,128)(2,1)S(1)}, bf16[26,128,256]{2,1,0:T(8,128)(2,1)}, u32[]{:S(2)}, u32[]{:S(2)}) collective-permute-start(bf16[26,128,256]{2,1,0:T(8,128)(2,1)S(1)} %get-tuple-element.39), channel_id=1, source_target_pairs={{1,7},{3,2},{5,3},{7,5},{2,0},{9,15},{11,10},{13,11},{15,13},{10,8... | collective-permute-start | bytes 5111816 | tf_op jit(solution)/shard_map/cond/branch_1_fun/ppermute | solution.py:371
  153.7 18.0 %collective-permute-done.2 = bf16[26,128,256]{2,1,0:T(8,128)(2,1)} collective-permute-done((bf16[26,128,256]{2,1,0:T(8,128)(2,1)S(1)}, bf16[26,128,256]{2,1,0:T(8,128)(2,1)}, u32[]{:S(2)}, u32[]{:S(2)}) %collective-permute-start.2) | collective-permute-done | bytes 1703968 | tf_op jit(solution)/shard_map/cond/branch_1_fun/ppermute | solution.py:371
  171.7 3.8 %collective-permute-done.3 = bf16[26,128,256]{2,1,0:T(8,128)(2,1)} collective-permute-done((bf16[26,128,256]{2,1,0:T(8,128)(2,1)S(1)}, bf16[26,128,256]{2,1,0:T(8,128)(2,1)}, u32[]{:S(2)}, u32[]{:S(2)}) %collective-permute-start.3) | collective-permute-done | bytes 1703968 | tf_op jit(solution)/shard_map/cond/branch_1_fun/ppermute | solution.py:371
  175.5 4.4 %fill_slots.1 = (f32[4,512,512]{2,1,0:T(8,128)}, f32[4,512,512]{2,1,0:T(8,128)}, f32[4,512,512]{2,1,0:T(8,128)}, f32[4,512,512]{2,1,0:T(8,128)}) custom-call(s32[8]{0:T(128)} %get-tuple-element.85.meta, bf16[26,128,256]{2,1,0:T(8,128)(2,1)} %get-tuple-element.100.refs_0_, ...), custom_call_target="tpu_custom_call", output_to_operand_aliasing={{0}: (3, {}), {1}: (4, {}), {2}: (5, {}), {3}: (6, {})} | custom-call | tf_op jit(solution)/shard_map/fill_slots/pallas_call | solution.py:347
  (21 shorter events, 3.5 us)
Async XLA Ops:
  4.8 29.5 %all-to-all-start = ((bf16[4,2,2,128,512]{4,3,2,1,0:T(8,128)(2,1)}), bf16[4,2,2,128,512]{4,3,2,1,0:T(8,128)(2,1)}, u32[]{:S(2)}, u32[]{:S(2)}) async-start(bf16[4,2,2,128,512]{4,3,2,1,0:T(8,128)(2,1)} %get-tuple-element.86), calls=%async_computation | async-start | bytes 4194304 | tf_op jit(solution)/shard_map/all_to_all | solution.py:392
  13.8 49.3 %collective-permute-start.23 = (bf16[4,2,2,128,512]{4,3,2,1,0:T(8,128)(2,1)}, bf16[4,2,2,128,512]{4,3,2,1,0:T(8,128)(2,1)}, u32[]{:S(2)}, u32[]{:S(2)}) collective-permute-start(bf16[4,2,2,128,512]{4,3,2,1,0:T(8,128)(2,1)} %get-tuple-element.93), channel_id=1, source_target_pairs={{0,8},{1,9},{2,10},{3,11},{4,12},{5,13},{6,14},{7,15},{8,16},{9,17... | collective-permute-start | bytes 6291464 | tf_op jit(solution)/shard_map/ppermute | solution.py:398
  15.8 98.4 %collective-permute-start.19 = (bf16[4,2,2,128,512]{4,3,2,1,0:T(8,128)(2,1)}, bf16[4,2,2,128,512]{4,3,2,1,0:T(8,128)(2,1)}, u32[]{:S(2)}, u32[]{:S(2)}) collective-permute-start(bf16[4,2,2,128,512]{4,3,2,1,0:T(8,128)(2,1)} %get-tuple-element.91), channel_id=1, source_target_pairs={{0,9},{1,8},{2,11},{3,10},{4,13},{5,12},{6,15},{7,14},{8,17},{9,16... | collective-permute-start | bytes 6291464 | tf_op jit(solution)/shard_map/ppermute | solution.py:399
  34.3 102.0 %collective-permute-start.18 = (bf16[4,2,2,128,512]{4,3,2,1,0:T(8,128)(2,1)}, bf16[4,2,2,128,512]{4,3,2,1,0:T(8,128)(2,1)}, u32[]{:S(2)}, u32[]{:S(2)}) collective-permute-start(bf16[4,2,2,128,512]{4,3,2,1,0:T(8,128)(2,1)} %all-to-all-done), channel_id=1, source_target_pairs={{0,1},{1,0},{2,3},{3,2},{4,5},{5,4},{6,7},{7,6},{8,9},{9,8},{10,11... | collective-permute-start | bytes 6291464 | tf_op jit(solution)/shard_map/ppermute | solution.py:402
  35.6 87.0 %all-to-all-start.1 = ((bf16[4,2,2,128,512]{4,3,2,1,0:T(8,128)(2,1)}), bf16[4,2,2,128,512]{4,3,2,1,0:T(8,128)(2,1)S(1)}, u32[]{:S(2)}, u32[]{:S(2)}) async-start(bf16[4,2,2,128,512]{4,3,2,1,0:T(8,128)(2,1)} %get-tuple-element.92), calls=%async_computation.1 | async-start | bytes 4194304 | tf_op jit(solution)/shard_map/all_to_all | solution.py:392
  65.4 55.8 %copy-start.4 = (s32[8]{0:T(128)S(1)}, s32[8]{0:T(128)}, u32[]{:S(2)}) copy-start(s32[8]{0:T(128)} %get-tuple-element.85.meta) | copy-start | bytes 100
  65.4 51.4 %collective-permute-start.24 = (bf16[1,2,2,128,512]{4,3,2,1,0:T(8,128)(2,1)S(1)}, bf16[1,2,2,128,512]{4,3,2,1,0:T(8,128)(2,1)S(1)}, u32[]{:S(2)}, u32[]{:S(2)}) collective-permute-start(bf16[1,2,2,128,512]{4,3,2,1,0:T(8,128)(2,1)S(1)} %get-tuple-element.112), channel_id=1, source_target_pairs={{0,2},{1,3},{2,4},{3,5},{4,6},{5,7},{6,0},{7,1},{8,10},{9,11},{10,... | collective-permute-start | bytes 1572872 | tf_op jit(solution)/shard_map/ppermute | solution.py:396
  65.5 54.9 %collective-permute-start.25 = (bf16[1,2,2,128,512]{4,3,2,1,0:T(8,128)(2,1)S(1)}, bf16[1,2,2,128,512]{4,3,2,1,0:T(8,128)(2,1)S(1)}, u32[]{:S(2)}, u32[]{:S(2)}) collective-permute-start(bf16[1,2,2,128,512]{4,3,2,1,0:T(8,128)(2,1)S(1)} %get-tuple-element.111), channel_id=1, source_target_pairs={{0,4},{1,5},{2,6},{3,7},{4,0},{5,1},{6,2},{7,3},{8,12},{9,13},{10,... | collective-permute-start | bytes 1572872 | tf_op jit(solution)/shard_map/ppermute | solution.py:396
  68.3 54.3 %collective-permute-start.26 = (bf16[1,2,2,128,512]{4,3,2,1,0:T(8,128)(2,1)}, bf16[1,2,2,128,512]{4,3,2,1,0:T(8,128)(2,1)}, u32[]{:S(2)}, u32[]{:S(2)}) collective-permute-start(bf16[1,2,2,128,512]{4,3,2,1,0:T(8,128)(2,1)} %get-tuple-element.110), channel_id=1, source_target_pairs={{0,6},{1,7},{2,0},{3,1},{4,2},{5,3},{6,4},{7,5},{8,14},{9,15},{10,... | collective-permute-start | bytes 1572872 | tf_op jit(solution)/shard_map/ppermute | solution.py:396
  116.7 16.8 %collective-permute-start.20 = (bf16[1,2,2,128,512]{4,3,2,1,0:T(8,128)(2,1)}, bf16[1,2,2,128,512]{4,3,2,1,0:T(8,128)(2,1)S(1)}, u32[]{:S(2)}, u32[]{:S(2)}) collective-permute-start(bf16[1,2,2,128,512]{4,3,2,1,0:T(8,128)(2,1)} %get-tuple-element.115), channel_id=1, source_target_pairs={{0,2},{1,3},{2,4},{3,5},{4,6},{5,7},{6,0},{7,1},{8,10},{9,11},{10,... | collective-permute-start | bytes 1572872 | tf_op jit(solution)/shard_map/ppermute | solution.py:396
  116.8 0.8 copy-start
  117.6 16.0 %collective-permute-start.21 = (bf16[1,2,2,128,512]{4,3,2,1,0:T(8,128)(2,1)}, bf16[1,2,2,128,512]{4,3,2,1,0:T(8,128)(2,1)S(1)}, u32[]{:S(2)}, u32[]{:S(2)}) collective-permute-start(bf16[1,2,2,128,512]{4,3,2,1,0:T(8,128)(2,1)} %get-tuple-element.114), channel_id=1, source_target_pairs={{0,4},{1,5},{2,6},{3,7},{4,0},{5,1},{6,2},{7,3},{8,12},{9,13},{10,... | collective-permute-start | bytes 1572872 | tf_op jit(solution)/shard_map/ppermute | solution.py:396
  120.4 0.8 copy-start.2
  121.2 15.1 %collective-permute-start.22 = (bf16[1,2,2,128,512]{4,3,2,1,0:T(8,128)(2,1)}, bf16[1,2,2,128,512]{4,3,2,1,0:T(8,128)(2,1)}, u32[]{:S(2)}, u32[]{:S(2)}) collective-permute-start(bf16[1,2,2,128,512]{4,3,2,1,0:T(8,128)(2,1)} %get-tuple-element.113), channel_id=1, source_target_pairs={{0,6},{1,7},{2,0},{3,1},{4,2},{5,3},{6,4},{7,5},{8,14},{9,15},{10,... | collective-permute-start | bytes 1572872 | tf_op jit(solution)/shard_map/ppermute | solution.py:396
  122.6 1.0 copy-start.1
  123.7 1.0 copy-start.3
  147.6 24.1 %collective-permute-start.2 = (bf16[26,128,256]{2,1,0:T(8,128)(2,1)S(1)}, bf16[26,128,256]{2,1,0:T(8,128)(2,1)}, u32[]{:S(2)}, u32[]{:S(2)}) collective-permute-start(bf16[26,128,256]{2,1,0:T(8,128)(2,1)S(1)} %get-tuple-element.38), channel_id=1, source_target_pairs={{1,0},{3,5},{5,7},{7,1},{9,8},{11,13},{13,15},{15,9},{17,16},{19,2... | collective-permute-start | bytes 5111816 | tf_op jit(solution)/shard_map/cond/branch_1_fun/ppermute | solution.py:371
  150.5 25.0 %collective-permute-start.3 = (bf16[26,128,256]{2,1,0:T(8,128)(2,1)S(1)}, bf16[26,128,256]{2,1,0:T(8,128)(2,1)}, u32[]{:S(2)}, u32[]{:S(2)}) collective-permute-start(bf16[26,128,256]{2,1,0:T(8,128)(2,1)S(1)} %get-tuple-element.39), channel_id=1, source_target_pairs={{1,7},{3,2},{5,3},{7,5},{2,0},{9,15},{11,10},{13,11},{15,13},{10,8... | collective-permute-start | bytes 5111816 | tf_op jit(solution)/shard_map/cond/branch_1_fun/ppermute | solution.py:371
